TPU v7x, 512 devices: a whole 4x4x16 slice. The times are simulated.
512 devices in a mesh: leaf: 32 (over z, core), front: 16 (over y, x).
Axes of the slice: x: 4, y: 4, z: 16, core: 2. Of those that a mesh axis runs over, the one named last changes fastest.
Arguments:
- parent_border_inverse: float32 [32, 1536, 1536], P('leaf', 'front')
- parent_border_rows: float32 [32, 1536, 768], P('leaf', 'front'), may hold values from -0.09 to 0.09
- parent_diagonal_inverse: float32 [32, 768, 768], P('leaf', 'front')
- child_border_rows: float32 [64, 1024, 512], P('leaf', 'front'), may hold values from -0.13 to 0.13
- child_factor_inverse: float32 [64, 512, 512], P('leaf', 'front')
- child_index: int32 [64, 1024], replicated, may hold values from 0 to 2303, as said below
- child_parent: int32 [64], replicated, may hold values from 0 to 31, as said below
Outputs:
- parent_variance: float32 [32, 768], P('leaf')
- child_variance: float32 [64, 512], P('leaf')
Inputs may be any that keep to these rules, and one draw needn't show every extreme that they name: `child_index`: each row holds 1024 distinct positions in increasing order, the first 0 and the last 2303. `child_parent`: child c's parent is c // 2 or c // 2 with its lowest bit flipped, and every parent has exactly two children.
All inputs are finite; a program needn't handle non-finite values.
Results may differ from a plain program's by a relative error of at most 0.0003.
Values sent between devices are 32-bit elements; how exact they have to be, the bound alone decides.
A program may use at most 64 MiB of HBM per device.

v0:
```python
import jax
import jax.numpy as jnp
from jax import lax
from jax.sharding import PartitionSpec as P

ELIMINATED_SIZE = 768
BORDER_SIZE = 1536
CHILD_ELIMINATED = 512


def partner_2(value, axis, distance):
    mask = 2**distance
    pairs = [(source, source ^ mask) for source in range(lax.axis_size(axis))]
    return lax.ppermute(value, axis, pairs)


def matrix_product(left, right):
    return jnp.dot(left, right, precision=lax.Precision.HIGHEST, preferred_element_type=jnp.float32)


def batched_fronts(form, left, right):
    return jnp.einsum(
        form, left, right, precision=lax.Precision.HIGHEST, preferred_element_type=jnp.float32
    )


def folded_rows(left_matrix, block_rows):
    return matrix_product(left_matrix, block_rows)


def children_of(child_parent, owner):
    partner = jnp.bitwise_xor(owner, 1)
    pool_ids = jnp.stack([2 * owner, 2 * owner + 1, 2 * partner, 2 * partner + 1])
    member = (jnp.take(child_parent, pool_ids) == owner).astype(jnp.int32)
    first = jnp.argmax(member)
    second = 3 - jnp.argmax(member[::-1])
    slots = jnp.stack([first, second])
    return (slots, jnp.take(pool_ids, slots))


def shards(
    parent_border_inverse,
    parent_border_rows,
    parent_diagonal_inverse,
    child_border_rows,
    child_factor_inverse,
    child_index,
    child_parent,
):
    border_inverse = parent_border_inverse[0]
    border_factor = parent_border_rows[0]
    eliminated_inverse = parent_diagonal_inverse[0]
    border_rows = border_inverse.shape[0]
    weight_rows = folded_rows(
        border_factor, lax.all_gather(eliminated_inverse, "front", axis=0, tiled=True)
    )
    own_weights = batched_fronts(
        "krj,kjm->krm",
        child_border_rows,
        lax.all_gather(child_factor_inverse, "front", axis=1, tiled=True),
    )
    leaf_index = lax.axis_index("leaf")
    partner = jnp.bitwise_xor(leaf_index, 1)
    partner_weights = partner_2(own_weights, "leaf", 0)
    pooled = jnp.concatenate([own_weights, partner_weights], axis=0)
    slots, kid_ids = children_of(child_parent, leaf_index)
    selected = jnp.take(pooled, slots, axis=0)
    child_weight = lax.all_gather(selected, "front", axis=1, tiled=True)
    index_list = jnp.take(child_index, kid_ids, axis=0)
    placed_rows = (
        jnp.zeros((2, ELIMINATED_SIZE + BORDER_SIZE, CHILD_ELIMINATED), jnp.float32)
        .at[jnp.arange(2)[:, None], index_list]
        .set(child_weight)
    )
    upper_block = placed_rows[:, :ELIMINATED_SIZE]
    lower_block = placed_rows[:, ELIMINATED_SIZE:]
    own_lower = lax.dynamic_slice_in_dim(
        lower_block, lax.axis_index("front") * border_rows, border_rows, 1
    )
    reduced = own_lower - batched_fronts("zt,qtg->qzg", weight_rows, upper_block)
    border_product = folded_rows(
        border_inverse, lax.all_gather(weight_rows, "front", axis=0, tiled=True)
    )
    parent_block = jnp.sum(eliminated_inverse * eliminated_inverse, axis=0) + jnp.sum(
        weight_rows * border_product, axis=0
    )
    kid_image = batched_fronts("rb,kbm->krm", border_inverse, lower_block) - batched_fronts(
        "zt,qtg->qzg", border_product, upper_block
    )
    lifted_rows = batched_fronts("zt,qtg->qzg", eliminated_inverse, upper_block)
    quad_part = jnp.sum(lifted_rows * lifted_rows, axis=1) + jnp.sum(reduced * kid_image, axis=1)
    own_part = jnp.sum(child_factor_inverse * child_factor_inverse, axis=1)
    parent_total, quad_total, own_total = lax.psum((parent_block, quad_part, own_part), "front")
    returned = partner_2(quad_total, "leaf", 0)
    partner_slots, partner_ids = children_of(child_parent, partner)
    mine = 2 * leaf_index + jnp.arange(2, dtype=jnp.int32)
    from_self = (kid_ids[None, :] == mine[:, None]).astype(jnp.float32)
    from_partner = (partner_ids[None, :] == mine[:, None]).astype(jnp.float32)
    kid_quadratic = matrix_product(from_self, quad_total) + matrix_product(from_partner, returned)
    return (parent_total[None], own_total + kid_quadratic)


def solution(mesh):
    in_specs = (
        P("leaf", "front", None),
        P("leaf", "front", None),
        P("leaf", "front", None),
        P("leaf", "front", None),
        P("leaf", "front", None),
        P(),
        P(),
    )
    out_specs = (P("leaf", None), P("leaf", None))
    return jax.shard_map(shards, mesh=mesh, in_specs=in_specs, out_specs=out_specs, check_vma=False)
```

profile of v0, /device:TPU:1, one launch (start us, length us, event | category | flops | bytes accessed | tf_op | source)
XLA Modules:
  0.0 379.8 jit_solution(9751702435656411364)
XLA Ops:
  7.2 0.7 all-gather.8.cloned.1.call-update
  8.0 0.7 all-gather.12.cloned.1.call-update
  8.9 1.4 gather_fusion.2
  10.3 0.7 iota_reduce_fusion.2
  11.6 0.7 iota_reduce_fusion.3
  12.4 62.6 %all-gather.8.cloned.1.call-done = f32[2,512,512]{2,1,0:T(8,128)} async-done(((f32[2,32,512]{2,1,0:T(8,128)}), f32[2,512,512]{2,1,0:T(8,128)}) %all-gather.8.cloned.1.call-update) | async-done | bytes 2097168 | tf_op jit(solution)/shard_map/all_gather | solution.py:60
  75.0 3.1 fusion.44
  78.1 4.1 %collective-permute-start = (f32[2,64,512]{2,1,0:T(8,128)S(1)}, f32[2,64,512]{2,1,0:T(8,128)S(1)}, u32[]{:S(2)}, u32[]{:S(2)}) collective-permute-start(f32[2,64,512]{2,1,0:T(8,128)S(1)} %fusion.44), channel_id=1, source_target_pairs={{0,16},{16,0},{32,48},{48,32},{64,80},{80,64},{96,112},{112,96},{1... | collective-permute-start | bytes 786440 | tf_op jit(solution)/shard_map/ppermute | solution.py:14
  82.2 0.8 fusion.38
  83.0 0.8 compare_and_fusion
  84.4 0.8 broadcast_select_fusion
  85.2 53.2 %all-gather.12.cloned.1.call-done = f32[1,768,768]{2,1,0:T(8,128)} async-done(((f32[1,48,768]{2,1,0:T(8,128)}), f32[1,768,768]{2,1,0:T(8,128)}) %all-gather.12.cloned.1.call-update) | async-done | bytes 2359312 | tf_op jit(solution)/shard_map/all_gather | solution.py:55
  138.5 3.9 %fusion.8 = f32[96,768]{1,0:T(8,128)} fusion(f32[1,768,768]{2,1,0:T(8,128)} %all-gather.12.cloned.1.call-done, f32[1,96,768]{2,1,0:T(8,128)S(1)} %copy-done.6), kind=kOutput, calls=%fused_computation.15 | convolution fusion | flops 679477248 | bytes 2949120 | tf_op jit(solution)/shard_map/dot_general | solution.py:18
  143.0 1.5 gather_fusion
  144.9 0.6 gather_fusion.4
  145.6 0.7 iota_reduce_fusion
  146.9 0.7 iota_reduce_fusion.1
  147.6 0.7 compare_select_fusion.1
  149.0 0.7 and_select_fusion
  149.7 59.2 %all-gather.10.cloned.1.call-done = f32[2,1024,512]{2,1,0:T(8,128)} async-done(((f32[2,64,512]{2,1,0:T(8,128)}), f32[2,1024,512]{2,1,0:T(8,128)}) %all-gather.10.cloned.1.call-update) | async-done | bytes 4194320 | tf_op jit(solution)/shard_map/all_gather | solution.py:68
  208.9 13.8 %scatter_custom_fusion = f32[4608,512]{1,0:T(8,128)} fusion(s32[2048]{0:T(1024)S(1)} %bitcast.76, f32[2048,512]{1,0:T(8,128)} %bitcast.77, f32[]{:T(128)} %constant.46.clone.1), kind=kCustom, calls=%fused_computation.7 | custom fusion | bytes 9437696
  222.7 3.7 slice.21
  226.4 1.8 copy-done.2
  228.2 2.1 fusion.22
  230.3 2.0 fusion.15
  232.3 48.3 %all-gather.6.cloned.1.call-done = f32[1536,768]{1,0:T(8,128)} async-done(((f32[96,768]{1,0:T(8,128)}), f32[1536,768]{1,0:T(8,128)}) %all-gather.6.cloned.1.call-update) | async-done | bytes 4718608 | tf_op jit(solution)/shard_map/all_gather | solution.py:82
  280.7 5.3 %fusion.31 = (f32[768]{0:T(1024)S(1)}, f32[768,96]{0,1:T(8,128)S(1)}) fusion(f32[96,768]{1,0:T(8,128)S(1)} %copy-done.3, f32[1536,768]{1,0:T(8,128)} %all-gather.6.cloned.1.call-done, f32[1,96,1536]{2,1,0:T(8,128)S(1)} %copy-done), kind=kOutput, calls=%fused_computation.34 | convolution fusion | flops 1359101184 | bytes 5901312 | tf_op jit(solution)/shard_map/dot_general | solution.py:18
  286.0 3.9 %fusion.2 = f32[2,512,96]{1,2,0:T(8,128)S(1)} fusion(f32[2,2304,512]{2,1,0:T(8,128)} %bitcast.72, f32[768,96]{0,1:T(8,128)S(1)} %get-tuple-element.24), kind=kOutput, calls=%fused_computation.9 | convolution fusion | flops 905969664 | bytes 3833856 | tf_op jit(solution)/shard_map/zt,qtg->qzg/dot_general | solution.py:22
  289.9 6.7 %fusion.21 = f32[2,512]{1,0:T(2,128)S(1)} fusion(f32[2,96,512]{2,1,0:T(8,128)S(1)} %fusion.15, f32[2,512,96]{1,2,0:T(8,128)S(1)} %fusion.2, f32[1,96,1536]{2,1,0:T(8,128)S(1)} %copy-done, f32[2,2304,512]{2,1,0:T(8,128)} %bitcast.73), kind=kOutput, calls=%fused_computation.23 | convolution fusion | flops 1812233216 | bytes 7671808 | tf_op jit(solution)/shard_map/rb,kbm->krm/dot_general | solution.py:22
  296.6 58.2 %all-reduce = (f32[1,768]{1,0:T(1,128)}, f32[2,512]{1,0:T(2,128)S(1)}, f32[2,512]{1,0:T(2,128)S(1)}) all-reduce(f32[1,768]{1,0:T(1,128)S(1)} %broadcast_in_dim.45, f32[2,512]{1,0:T(2,128)S(1)} %multiply_reduce_fusion, f32[2,512]{1,0:T(2,128)S(1)} %add.91), channel_id=1, replica_groups=mesh['leaf'=32,'front'=16] {'front'}, use_global_device_ids=true, to_apply=%region_2.3 | all-reduce | flops 2816 | bytes 22528 | tf_op jit(solution)/shard_map/psum | solution.py:93
  354.8 16.9 %collective-permute-start.1 = (f32[2,512]{1,0:T(2,128)S(1)}, f32[2,512]{1,0:T(2,128)S(1)}, u32[]{:S(2)}, u32[]{:S(2)}) collective-permute-start(f32[2,512]{1,0:T(2,128)S(1)} %get-tuple-element.14), channel_id=1, source_target_pairs={{0,16},{16,0},{32,48},{48,32},{64,80},{80,64},{96,112},{112,96},{1... | collective-permute-start | bytes 12296 | tf_op jit(solution)/shard_map/ppermute | solution.py:14
  372.5 0.8 fusion.25
  (55 shorter events, 3.6 us)
Async XLA Ops:
  7.2 273.5 %copy-start = (f32[1,96,1536]{2,1,0:T(8,128)S(1)}, f32[1,96,1536]{2,1,0:T(8,128)}, u32[]{:S(2)}) copy-start(f32[1,96,1536]{2,1,0:T(8,128)} %param.11) | copy-start | bytes 1769476
  7.2 131.3 %copy-start.6 = (f32[1,96,768]{2,1,0:T(8,128)S(1)}, f32[1,96,768]{2,1,0:T(8,128)}, u32[]{:S(2)}) copy-start(f32[1,96,768]{2,1,0:T(8,128)} %param.12) | copy-start | bytes 884740
  7.2 67.8 %all-gather.8.cloned.1.call-start = ((), (), s32[]{:S(2)}) async-start(), calls=%async_computation.1 | async-start | bytes 2228224 | tf_op jit(solution)/shard_map/all_gather | solution.py:60
  7.9 130.5 %all-gather.12.cloned.1.call-start = ((), (), s32[]{:S(2)}) async-start(), calls=%async_computation.3 | async-start | bytes 2506752 | tf_op jit(solution)/shard_map/all_gather | solution.py:55
  8.7 200.2 %all-gather.10.cloned.1.call-start = ((), (), s32[]{:S(2)}) async-start(), calls=%async_computation.2 | async-start | bytes 4456448 | tf_op jit(solution)/shard_map/all_gather | solution.py:68
  8.8 135.8 %copy-start.7 = (s32[2]{0:T(128)S(1)}, s32[2]{0:T(128)}, u32[]{:S(2)}) copy-start(s32[2]{0:T(128)} %constant.94) | copy-start | bytes 28
  8.8 135.9 %copy-start.8 = (s32[2]{0:T(128)S(1)}, s32[2]{0:T(128)}, u32[]{:S(2)}) copy-start(s32[2]{0:T(128)} %constant.97) | copy-start | bytes 28
  8.8 136.0 %copy-start.1 = (s32[64]{0:T(128)S(1)}, s32[64]{0:T(128)}, u32[]{:S(2)}) copy-start(s32[64]{0:T(128)} %param.17) | copy-start | bytes 772
  12.4 136.6 %copy-start.5 = (f32[2,32,512]{2,1,0:T(8,128)S(1)}, f32[2,32,512]{2,1,0:T(8,128)}, u32[]{:S(2)}) copy-start(f32[2,32,512]{2,1,0:T(8,128)} %param.15) | copy-start | bytes 393220
  12.4 136.6 %copy-start.4 = (f32[1,48,768]{2,1,0:T(8,128)S(1)}, f32[1,48,768]{2,1,0:T(8,128)}, u32[]{:S(2)}) copy-start(f32[1,48,768]{2,1,0:T(8,128)} %param.13) | copy-start | bytes 442372
  78.1 5.7 %collective-permute-start = (f32[2,64,512]{2,1,0:T(8,128)S(1)}, f32[2,64,512]{2,1,0:T(8,128)S(1)}, u32[]{:S(2)}, u32[]{:S(2)}) collective-permute-start(f32[2,64,512]{2,1,0:T(8,128)S(1)} %fusion.44), channel_id=1, source_target_pairs={{0,16},{16,0},{32,48},{48,32},{64,80},{80,64},{96,112},{112,96},{1... | collective-permute-start | bytes 786440 | tf_op jit(solution)/shard_map/ppermute | solution.py:14
  85.2 195.5 %all-gather.6.cloned.1.call-start = ((), (), s32[]{:S(2)}) async-start(), calls=%async_computation | async-start | bytes 5013504 | tf_op jit(solution)/shard_map/all_gather | solution.py:82
  222.7 5.5 %copy-start.2 = (f32[4608,512]{1,0:T(8,128)S(1)}, f32[4608,512]{1,0:T(8,128)}, u32[]{:S(2)}) copy-start(f32[4608,512]{1,0:T(8,128)} %scatter_custom_fusion) | copy-start | bytes 28311556
  222.7 7.6 %copy-start.3 = (f32[96,768]{1,0:T(8,128)S(1)}, f32[96,768]{1,0:T(8,128)}, u32[]{:S(2)}) copy-start(f32[96,768]{1,0:T(8,128)} %fusion.8) | copy-start | bytes 884740
  354.8 17.7 %collective-permute-start.1 = (f32[2,512]{1,0:T(2,128)S(1)}, f32[2,512]{1,0:T(2,128)S(1)}, u32[]{:S(2)}, u32[]{:S(2)}) collective-permute-start(f32[2,512]{1,0:T(2,128)S(1)} %get-tuple-element.14), channel_id=1, source_target_pairs={{0,16},{16,0},{32,48},{48,32},{64,80},{80,64},{96,112},{112,96},{1... | collective-permute-start | bytes 12296 | tf_op jit(solution)/shard_map/ppermute | solution.py:14
Sparse Core Ops, SparseCore 0:
  11.0 63.9 all-gather.7
  78.0 60.4 all-gather.11
  141.5 67.3 all-gather.9
  211.7 68.8 all-gather.5
where the time goes:
time: 380 us
  waiting for transfers between devices  225 us (59%)
  blocking collectives  58.2 us (15%)
  matrix products  27.9 us (7%)
  local copies, waits for them, and re-layouts  24.9 us (7%)
  starting transfers between devices  21.2 us (6%)
  between operations  15.3 us (4%)
  other arithmetic  6.92 us (2%)
    all_gather x1, waiting for transfers between devices, shards(): lax.all_gather(child_factor_inverse, 'front', axis=1, tiled=True)  62.6 us
    all_gather x1, waiting for transfers between devices, shards(): child_weight = lax.all_gather(selected, 'front', axis=1, tiled=True)  59.2 us
    psum x1, blocking collectives, shards(): lax.psum((parent_block, quad_part, own_part), 'front')  58.2 us
    all_gather x1, waiting for transfers between devices, shards(): lax.all_gather(eliminated_inverse, 'front', axis=0, tiled=True)  53.2 us
    all_gather x1, waiting for transfers between devices, shards(): lax.all_gather(weight_rows, 'front', axis=0, tiled=True)  48.3 us
    ppermute x2, starting transfers between devices, partner_2(): return lax.ppermute(value, axis, pairs)  21 us
    dot_general x5, matrix products, batched_fronts(): jnp.einsum(form, left, right, precision=lax.Precision.HIGHEST, preferred_...  17.8 us
    unnamed x20, local copies, waits for them, and re-layouts  15.7 us
  transfers between devices with their start and end apart: 6, of which 5 were waited for; matrix products, arithmetic and copies ran while one was open for 11% of the time, Pallas kernels for 0%

commit v1 on v0

v1 whole, which is shorter than its diff:
```python
import jax
import jax.numpy as jnp
from jax import lax
from jax.experimental import pallas as pl
from jax.experimental.pallas import tpu as pltpu
from jax.sharding import PartitionSpec as P

F32 = jnp.float32
BF16 = jnp.bfloat16
MESH = pl.DeviceIdType.MESH


def dot(a, b):
    return jnp.dot(a, b, preferred_element_type=F32)


def dot3(ah, al, bh, bl):
    return dot(ah, bh) + (dot(ah, bl) + dot(al, bh))


def split(x):
    hi = x.astype(BF16)
    return hi, (x - hi.astype(F32)).astype(BF16)


def col_sum(x):
    return jnp.sum(x, axis=0, keepdims=True)


def select(flag, yes, no):
    return jnp.where(jnp.full(yes.shape, flag, jnp.int32) == 1, yes, no)


def kernel(
    b_in, f_in, d_in, cf_in, e_in, idx_in, owner,
    out_p, out_c,
    b_s, f_s, d_s, cf_s, e_s, k_own, k_par, k_s, v_s, r_s, idx_s, l_s,
    su, sl, bh, bl, fh, fl, dh, dl, ch, cl, eh, el, kh, kl, uh, ul, vh, vl, rh, rl,
    stage, fin, ostage, xfin, send, recv, loc,
):
    leaf = lax.axis_index("leaf")
    front = lax.axis_index("front")
    y = lax.div(front, 4)
    x = lax.rem(front, 4)
    partner = leaf + 1 - 2 * lax.rem(leaf, 2)
    count = [0]
    copies = []

    def remote(src, dst, device):
        k = count[0]
        count[0] += 1
        copy = pltpu.make_async_remote_copy(
            src_ref=src, dst_ref=dst, send_sem=send.at[k], recv_sem=recv.at[k],
            device_id=device, device_id_type=MESH,
        )
        copies.append(copy)
        return copy

    def at_x(p):
        return {"front": y * 4 + p}

    def at_y(p):
        return {"front": p * 4 + x}

    class Ring:
        def __init__(self, device, pos, slot, half, own=None):
            right, left = lax.rem(pos + 1, 4), lax.rem(pos + 3, 4)
            own = slot(pos) if own is None else own
            self.first_r = remote(own, slot(pos), device(right))
            self.first_l = remote(own, slot(pos), device(left))
            self.next_r = remote(half(left, 0), half(left, 0), device(right))
            self.next_l = remote(half(right, 1), half(right, 1), device(left))

        def begin(self):
            self.first_r.start()
            self.first_l.start()

        def relay(self):
            self.first_r.wait_recv()
            self.next_r.start()
            self.first_l.wait_recv()
            self.next_l.start()

        def finish(self):
            self.next_r.wait_recv()
            self.next_l.wait_recv()

    def rows(ref, size):
        return lambda p: ref.at[pl.ds(p * size, size), :]

    def half_rows(ref, size):
        return lambda p, h: ref.at[pl.ds(p * size + h * (size // 2), size // 2), :]

    def stacked(ref, base, size):
        return lambda p: ref.at[pl.ds(base, 2), pl.ds(p * size, size), :]

    def half_stacked(ref, base, size):
        return lambda p, h: ref.at[base + h, pl.ds(p * size, size), :]

    def tile(ref, t, size):
        return lambda p: ref.at[t, pl.ds(p * size, size), :]

    def half_tile(ref, t, size):
        return lambda p, h: ref.at[t, pl.ds(p * size + h * (size // 2), size // 2), :]

    barrier = pltpu.get_barrier_semaphore()
    peers = [at_x(lax.rem(x + d, 4)) for d in (1, 2, 3)]
    peers += [at_y(lax.rem(y + d, 4)) for d in (1, 2, 3)]
    peers += [
        {"leaf": partner, "front": lax.rem(y + d, 4) * 4 + x} for d in (0, 1, 2, 3)
    ]
    for peer in peers:
        pl.semaphore_signal(barrier, inc=1, device_id=peer, device_id_type=MESH)

    locals_ = [
        (e_in.at[:, :, pl.ds(pl.multiple_of(x * 128, 128), 128)], e_s.at[:, pl.ds(y * 128 + x * 32, 32), :]),
        (d_in, d_s.at[pl.ds(x * 48, 48), :]),
        (cf_in, cf_s.at[:, pl.ds(x * 64, 64), :]),
        (f_in, f_s.at[pl.ds(x * 96, 96), :]),
        (b_in, b_s.at[pl.ds(x * 96, 96), :]),
        (idx_in.at[pl.ds(pl.multiple_of(lax.div(leaf, 4) * 8, 8), 8), :], idx_s),
    ]
    own_e, own_d, own_cf, own_f, own_b, own_idx = [
        pltpu.make_async_copy(src, dst, loc.at[i]) for i, (src, dst) in enumerate(locals_)
    ]
    for copy in (own_e, own_d, own_cf, own_f, own_b, own_idx):
        copy.start()

    e_across = []
    for d in (1, 2, 3):
        other = lax.rem(x + d, 4)
        e_across.append(remote(
            e_in.at[:, :, pl.ds(pl.multiple_of(other * 128, 128), 128)],
            e_s.at[:, pl.ds(y * 128 + x * 32, 32), :],
            at_x(other),
        ))
    ring_d = Ring(at_x, x, rows(d_s, 48), half_rows(d_s, 48), d_in)
    ring_cf = Ring(at_x, x, stacked(cf_s, 0, 64), half_stacked(cf_s, 0, 64), cf_in)
    ring_f = Ring(at_x, x, rows(f_s, 96), half_rows(f_s, 96), f_in)
    ring_b = Ring(at_x, x, rows(b_s, 96), half_rows(b_s, 96), b_in)
    ring_e = Ring(at_y, y, stacked(e_s, 0, 128), half_stacked(e_s, 0, 128))
    ring_dp = Ring(at_y, y, stacked(v_s, 0, 192), half_stacked(v_s, 0, 192))
    ring_k = Ring(at_y, y, stacked(k_s, 0, 256), half_stacked(k_s, 0, 256))
    ring_v = Ring(at_y, y, stacked(v_s, 2, 192), half_stacked(v_s, 2, 192))
    ring_w0 = Ring(at_y, y, tile(r_s, 0, 384), half_tile(r_s, 0, 384))
    ring_w1 = Ring(at_y, y, tile(r_s, 1, 384), half_tile(r_s, 1, 384))
    ring_r = Ring(at_y, y, stacked(r_s, 2, 384), half_stacked(r_s, 2, 384))
    k_cross = remote(k_own, k_par, {"leaf": partner})

    pl.semaphore_wait(barrier, 10)

    for copy in e_across:
        copy.start()
    ring_d.begin()
    ring_cf.begin()

    pool = (2 * leaf, 2 * leaf + 1, 2 * partner, 2 * partner + 1)
    mine = [(owner[p] == leaf).astype(jnp.int32) for p in pool]
    theirs = [1 - m for m in mine]
    own_idx.wait()
    in_eight = [lax.rem(p, 8) for p in pool]
    idx_rows = [idx_s[pl.ds(p, 1), :] for p in in_eight]
    first_idx = select(mine[0], idx_rows[0], select(mine[1], idx_rows[1], idx_rows[2]))
    last_idx = select(mine[3], idx_rows[3], select(mine[2], idx_rows[2], idx_rows[1]))

    def one_hot(c, positions):
        for m in range(0, 768, 128):
            at = lax.broadcasted_iota(jnp.int32, (128, 1024), 0) + m
            su[c, pl.ds(m, 128), :] = jnp.where(at == positions, 1.0, 0.0).astype(BF16)
        for m in range(0, 384, 128):
            at = lax.broadcasted_iota(jnp.int32, (128, 1024), 0) + (768 + 384 * y + m)
            sl[c, pl.ds(m, 128), :] = jnp.where(at == positions, 1.0, 0.0).astype(BF16)

    def split_rows(src, hi, lo, size, step):
        for m in range(0, size, step):
            h, l = split(src[pl.ds(m, step), :])
            hi[pl.ds(m, step), :] = h
            lo[pl.ds(m, step), :] = l

    own_e.wait()
    for copy in e_across:
        copy.wait_recv()
    ring_e.begin()
    one_hot(0, first_idx)
    ring_d.relay()
    ring_e.relay()
    one_hot(1, last_idx)
    ring_cf.relay()
    ring_f.begin()

    own_d.wait()
    ring_d.finish()
    window = (x + lax.div(x, 2)) * 128
    d_sums = []
    for t in range(2):
        part = d_s[:, pl.ds(pl.multiple_of(window + t * 128, 128), 128)]
        v_s[t, pl.ds(pl.multiple_of(y * 192, 192), 192), :] = part
        d_sums.append(col_sum(part * part))
    ring_dp.begin()
    split_rows(d_s, dh, dl, 192, 48)

    ring_e.finish()
    e_sums = []
    for c in range(2):
        for m in range(0, 512, 128):
            h, l = split(e_s[c, pl.ds(m, 128), :])
            eh[c, pl.ds(m, 128), :] = h
            el[c, pl.ds(m, 128), :] = l
        part = e_s[c, pl.ds(pl.multiple_of(y * 128, 128), 128), :]
        e_sums.append(col_sum(part * part))
    own_cf.wait()
    ring_cf.finish()
    for c in range(2):
        for m in range(0, 256, 64):
            h, l = split(cf_s[c, pl.ds(m, 64), :])
            ch[c, pl.ds(m, 64), :] = h
            cl[c, pl.ds(m, 64), :] = l
        for m in range(0, 256, 128):
            at = pl.ds(m, 128)
            k_own[c, at, :] = dot3(ch[c, at, :], cl[c, at, :], eh[c], el[c])
    k_cross.start()
    ring_dp.relay()
    k_cross.wait_recv()
    for m in range(0, 256, 64):
        at = pl.ds(m, 64)
        pooled = [k_own[0, at, :], k_own[1, at, :], k_par[0, at, :], k_par[1, at, :]]
        to = pl.ds(pl.multiple_of(y * 256 + m, 64), 64)
        k_s[0, to, :] = select(mine[0], pooled[0], select(mine[1], pooled[1], pooled[2]))
        k_s[1, to, :] = select(mine[3], pooled[3], select(mine[2], pooled[2], pooled[1]))
    ring_k.begin()
    ring_f.relay()
    ring_b.begin()

    def split_v(base):
        for t in range(2):
            for m in range(0, 768, 128):
                h, l = split(v_s[base + t, pl.ds(m, 128), :])
                vh[pl.ds(m, 128), pl.ds(t * 128, 128)] = h
                vl[pl.ds(m, 128), pl.ds(t * 128, 128)] = l

    ring_dp.finish()
    split_v(0)
    ring_k.relay()
    own_f.wait()
    ring_f.finish()
    split_rows(f_s, fh, fl, 384, 48)
    for m in range(0, 384, 128):
        at = pl.ds(m, 128)
        value = dot3(fh[at, :], fl[at, :], vh[...], vl[...])
        to = pl.ds(pl.multiple_of(y * 384 + m, 128), 128)
        r_s[0, to, :] = value[:, :128]
        r_s[1, to, :] = value[:, 128:]
    ring_w0.begin()

    ring_k.finish()
    for c in range(2):
        for m in range(0, 1024, 128):
            h, l = split(k_s[c, pl.ds(m, 128), :])
            kh[c, pl.ds(m, 128), :] = h
            kl[c, pl.ds(m, 128), :] = l
        for m in range(0, 768, 256):
            at = pl.ds(m, 256)
            uh[at, pl.ds(c * 128, 128)] = dot(su[c, at, :], kh[c]).astype(BF16)
            ul[at, pl.ds(c * 128, 128)] = dot(su[c, at, :], kl[c]).astype(BF16)
    v_sums = [jnp.zeros((1, 128), F32)] * 2
    for m in range(0, 192, 96):
        at = pl.ds(m, 96)
        value = dot3(dh[at, :], dl[at, :], uh[...], ul[...])
        to = pl.ds(pl.multiple_of(y * 192 + m, 96), 96)
        for c in range(2):
            part = value[:, c * 128:(c + 1) * 128]
            v_s[2 + c, to, :] = part
            v_sums[c] = v_sums[c] + col_sum(part * part)
    ring_v.begin()
    ring_w0.relay()
    ring_v.relay()
    ring_w1.begin()
    for c in range(2):
        for m in range(0, 384, 128):
            at = pl.ds(m, 128)
            l_s[at, pl.ds(c * 128, 128)] = dot(sl[c, at, :], kh[c]) + dot(sl[c, at, :], kl[c])
    ring_b.relay()
    ring_v.finish()
    split_v(2)
    for m in range(0, 384, 128):
        at = pl.ds(m, 128)
        value = l_s[at, :] - dot3(fh[at, :], fl[at, :], vh[...], vl[...])
        to = pl.ds(pl.multiple_of(y * 384 + m, 128), 128)
        r_s[2, to, :] = value[:, :128]
        r_s[3, to, :] = value[:, 128:]
    ring_r.begin()
    ring_w1.relay()
    own_b.wait()
    ring_b.finish()
    split_rows(b_s, bh, bl, 384, 24)
    ring_r.relay()

    def quadratic(base):
        for t in range(2):
            for m in range(0, 1536, 128):
                h, l = split(r_s[base + t, pl.ds(m, 128), :])
                rh[pl.ds(m, 128), pl.ds(t * 128, 128)] = h
                rl[pl.ds(m, 128), pl.ds(t * 128, 128)] = l
        sums = [jnp.zeros((1, 128), F32)] * 2
        for m in range(0, 384, 128):
            at = pl.ds(m, 128)
            value = dot3(bh[at, :], bl[at, :], rh[...], rl[...])
            to = pl.ds(pl.multiple_of(y * 384 + m, 128), 128)
            for t in range(2):
                sums[t] = sums[t] + col_sum(value[:, t * 128:(t + 1) * 128] * r_s[base + t, to, :])
        return sums

    ring_w0.finish()
    ring_w1.finish()
    p_sums = quadratic(0)
    ring_r.finish()
    c_sums = quadratic(2)

    for t in range(2):
        stage[pl.ds(t, 1), :] = p_sums[t] + d_sums[t]
        stage[pl.ds(2 + t, 1), :] = c_sums[t] + v_sums[t]
        stage[pl.ds(4 + t, 1), :] = e_sums[t]
    stage[pl.ds(6, 2), :] = jnp.zeros((2, 128), F32)
    fin[0, y] = stage[...]
    ends = []
    for d in (1, 2, 3):
        ends.append(remote(stage, fin.at[0, y], at_y(lax.rem(y + d, 4))))
    for d in (0, 1, 2, 3):
        ends.append(remote(stage, fin.at[1, y], {"leaf": partner, "front": lax.rem(y + d, 4) * 4 + x}))
    for copy in ends:
        copy.start()
    for copy in ends:
        copy.wait_recv()
    own = ((fin[0, 0] + fin[0, 1]) + fin[0, 2]) + fin[0, 3]
    other = ((fin[1, 0] + fin[1, 1]) + fin[1, 2]) + fin[1, 3]
    before = theirs[2] * 0 + (1 - mine[2]) + (1 - mine[3])
    quad_0 = select(mine[0], own[2:3], select(before, other[3:4], other[2:3]))
    quad_1 = select(mine[1], select(mine[0], own[3:4], own[2:3]), other[3:4])
    ostage[0:2, :] = own[0:2]
    ostage[2:3, :] = own[4:5] + quad_0
    ostage[3:4, :] = own[5:6] + quad_1
    ostage[4:8, :] = jnp.zeros((4, 128), F32)
    xfin[x] = ostage[...]
    ends = []
    for d in (1, 2, 3):
        ends.append(remote(ostage, xfin.at[x], at_x(lax.rem(x + d, 4))))
    for copy in ends:
        copy.start()
    for copy in ends:
        copy.wait_recv()
    for t, (p, r) in enumerate(((0, 0), (0, 1), (1, 1), (2, 0), (2, 1), (3, 1))):
        out_p[:, t * 128:(t + 1) * 128] = xfin[p, r:r + 1, :]
    for p in range(4):
        out_c[:, p * 128:(p + 1) * 128] = xfin[p, 2:4, :]
    for copy in copies:
        copy.wait_send()


COPIES = 58


def shards(b, f, d, cf, e, idx, owner):
    vm = pltpu.VMEM
    any_spec = pl.BlockSpec(memory_space=pl.ANY)
    vmem_spec = pl.BlockSpec(memory_space=pltpu.VMEM)
    return pl.pallas_call(
        kernel,
        out_shape=(jax.ShapeDtypeStruct((1, 768), F32), jax.ShapeDtypeStruct((2, 512), F32)),
        in_specs=[any_spec] * 6 + [pl.BlockSpec(memory_space=pltpu.SMEM)],
        out_specs=(vmem_spec, vmem_spec),
        scratch_shapes=[
            vm((384, 1536), F32), vm((384, 768), F32), vm((192, 768), F32),
            vm((2, 256, 512), F32), vm((2, 512, 128), F32),
            vm((2, 256, 128), F32), vm((2, 256, 128), F32), vm((2, 1024, 128), F32),
            vm((4, 768, 128), F32), vm((4, 1536, 128), F32), vm((8, 1024), jnp.int32),
            vm((384, 256), F32),
            vm((2, 768, 1024), BF16), vm((2, 384, 1024), BF16),
            vm((384, 1536), BF16), vm((384, 1536), BF16),
            vm((384, 768), BF16), vm((384, 768), BF16),
            vm((192, 768), BF16), vm((192, 768), BF16),
            vm((2, 256, 512), BF16), vm((2, 256, 512), BF16),
            vm((2, 512, 128), BF16), vm((2, 512, 128), BF16),
            vm((2, 1024, 128), BF16), vm((2, 1024, 128), BF16),
            vm((768, 256), BF16), vm((768, 256), BF16),
            vm((768, 256), BF16), vm((768, 256), BF16),
            vm((1536, 256), BF16), vm((1536, 256), BF16),
            vm((8, 128), F32), vm((2, 4, 8, 128), F32), vm((8, 128), F32), vm((4, 8, 128), F32),
            pltpu.SemaphoreType.DMA((COPIES,)),
            pltpu.SemaphoreType.DMA((COPIES,)),
            pltpu.SemaphoreType.DMA((6,)),
        ],
        compiler_params=pltpu.CompilerParams(
            collective_id=0, has_side_effects=True, vmem_limit_bytes=60 * 1024 * 1024
        ),
        name="selected",
    )(b[0], f[0], d[0], cf, e, idx, owner)


def solution(mesh):
    split_spec = P("leaf", "front", None)
    in_specs = (split_spec,) * 5 + (P(), P())
    out_specs = (P("leaf", None), P("leaf", None))
    return jax.shard_map(shards, mesh=mesh, in_specs=in_specs, out_specs=out_specs, check_vma=False)
```

time: 380 us -> 88.7 us (0.23)
  waiting for transfers between devices: 225 us -> 0 us
  Pallas kernels: 0 us -> 86 us
  blocking collectives: 58.2 us -> 0 us
  matrix products: 27.9 us -> 0 us
  local copies, waits for them, and re-layouts: 24.9 us -> 1.83 us
  starting transfers between devices: 21.2 us -> 0 us
  between operations: 15.3 us -> 0.66 us
  other arithmetic: 6.92 us -> 0 us
    all_gather x4 -> x0, waiting for transfers between devices: 223 us -> none  [the longest x1 62.6 us: shards(): lax.all_gather(child_factor_inverse, 'front', axis=1, tiled=True)]
    pallas_call x0 -> x1, Pallas kernels: none -> 86 us  [shards(): pl.pallas_call(kernel, out_shape=(jax.ShapeDtypeStruct((1, 768), F32), ja...]
    psum x1 -> x0, blocking collectives: 58.2 us -> none  [shards(): lax.psum((parent_block, quad_part, own_part), 'front')]
    dot_general x9 -> x0, matrix products: 27.9 us -> none  [the longest x5 17.8 us: batched_fronts(): jnp.einsum(form, left, right, precision=lax.Precision.HIGHEST, preferred_...]
    ppermute x2 -> x0, starting transfers between devices: 21 us -> none  [partner_2(): return lax.ppermute(value, axis, pairs)]
    unnamed x20 -> x6, local copies, waits for them, and re-layouts: 15.7 us -> 1.83 us
    gather x6 -> x0, local copies, waits for them, and re-layouts: 5.35 us -> none  [the longest x2 2 us: children_of(): member = (jnp.take(child_parent, pool_ids) == owner).astype(jnp.int32)]
  transfers between devices with their start and end apart: 6 -> 0, of which waited for: 5 -> 0; matrix products, arithmetic and copies ran while one was open for 11% -> 0% of each run, Pallas kernels for 0% -> 0%
where the time goes in v1:
time: 88.7 us; the launch traced here: 88.5 us
  Pallas kernels  86 us (97%)
  local copies, waits for them, and re-layouts  1.83 us (2%)
    pallas_call x1, Pallas kernels, shards(): pl.pallas_call(kernel, out_shape=(jax.ShapeDtypeStruct((1, 768), F32), ja...  86 us
    unnamed x6, local copies, waits for them, and re-layouts  1.83 us

profile of v1, /device:TPU:1, one launch (start us, length us, event | category | flops | bytes accessed | tf_op | source)
XLA Modules:
  0.0 88.5 jit_solution(4622334663348439540)
XLA Ops:
  0.6 86.0 %selected.1 = (f32[1,768]{1,0:T(1,128)}, f32[2,512]{1,0:T(2,128)}) custom-call(f32[96,1536]{1,0:T(8,128)} %bitcast.3, f32[96,768]{1,0:T(8,128)} %bitcast.4, f32[48,768]{1,0:T(8,128)} %bitcast.5, f32[2,64,512]{2,1,0:T(8,128)} %cf_in.1, f32[2,32,512]{2,1,0:T(8,128)} %e_in.1, s32[64,1024]{1,0:T(8,128)} %idx_in.1, s32[64]{0:T(128)} %owner.1), custom_call_target="tpu_custom_call" | custom-call | tf_op jit(solution)/shard_map/selected/pallas_call | solution.py:366
  86.7 0.0 copy-start.1
  86.7 0.0 copy-start
  86.7 0.7 copy-done.1
  87.3 0.6 copy.11
  87.9 0.0 copy-done
  87.9 0.6 copy.12
Async XLA Ops:
  86.7 0.7 copy-start.1
  86.7 1.2 %copy-start = (f32[2,512]{1,0:T(2,128)S(1)}, f32[2,512]{1,0:T(2,128)}, u32[]{:S(2)}) copy-start(f32[2,512]{1,0:T(2,128)} %get-tuple-element.5) | copy-start | bytes 12292

commit v2 on v1

v2 whole, which is shorter than its diff:
```python
import jax
import jax.numpy as jnp
from jax import lax
from jax.experimental import pallas as pl
from jax.experimental.pallas import tpu as pltpu
from jax.sharding import PartitionSpec as P

F32 = jnp.float32
BF16 = jnp.bfloat16
MESH = pl.DeviceIdType.MESH


def dot(a, b):
    return jnp.dot(a, b, preferred_element_type=F32)


def dot3(ah, al, bh, bl):
    return dot(ah, bh) + (dot(ah, bl) + dot(al, bh))


def split(x):
    hi = x.astype(BF16)
    return hi, (x - hi.astype(F32)).astype(BF16)


def col_sum(x):
    return jnp.sum(x, axis=0, keepdims=True)


def select(flag, yes, no):
    return jnp.where(jnp.full(yes.shape, flag, jnp.int32) == 1, yes, no)


def kernel(
    b_in, f_in, d_in, cf_in, e_in, idx_in, owner_in,
    out,
    b_s, f_s, d_s, cf_s, e_s, dp_s, k_own, k_par, k_s, v_s, v_pack, r_s, w_half, w_pack,
    idx_s, l_s, acc, owner,
    su, sl, bh, bl, fh, fl, dh, dl, ch, cl, eh, el, kh, kl, uh, ul, vh, vl, rh, rl,
    stage, fin, ostage, xfin, send, recv, loc,
):
    leaf = lax.axis_index("leaf")
    front = lax.axis_index("front")
    y = lax.div(front, 4)
    x = lax.rem(front, 4)
    partner = leaf + 1 - 2 * lax.rem(leaf, 2)
    copies = []

    def remote(src, dst, device):
        k = len(copies)
        copy = pltpu.make_async_remote_copy(
            src_ref=src, dst_ref=dst, send_sem=send.at[k], recv_sem=recv.at[k],
            device_id=device, device_id_type=MESH,
        )
        copies.append(copy)
        return copy

    def at_x(p):
        return {"front": y * 4 + p}

    def at_y(p):
        return {"front": p * 4 + x}

    class Ring:
        def __init__(self, device, pos, part, src=None):
            right, left = lax.rem(pos + 1, 4), lax.rem(pos + 3, 4)
            src = src or (lambda h: part(pos, h))
            self.right = [remote(src(h), part(pos, h), device(right)) for h in (0, 1)]
            self.left = [remote(src(h), part(pos, h), device(left)) for h in (1, 0)]
            self.next_right = remote(part(left, 0), part(left, 0), device(right))
            self.next_left = remote(part(right, 1), part(right, 1), device(left))

        def begin(self):
            for h in range(2):
                self.right[h].start()
                self.left[h].start()

        def relay(self):
            self.right[0].wait_recv()
            self.next_right.start()
            self.left[0].wait_recv()
            self.next_left.start()

        def near(self):
            self.right[1].wait_recv()
            self.left[1].wait_recv()

        def far(self):
            self.next_right.wait_recv()
            self.next_left.wait_recv()

        def finish(self):
            self.near()
            self.far()

    def halves(ref, size, *lead):
        return lambda p, h: ref.at[(*lead, pl.ds(p * size + h * (size // 2), size // 2), slice(None))]

    def of(ref, size):
        return lambda h: ref.at[pl.ds(h * (size // 2), size // 2), :]

    barrier = pltpu.get_barrier_semaphore()
    peers = [at_x(lax.rem(x + d, 4)) for d in (1, 2, 3)]
    peers += [at_y(lax.rem(y + d, 4)) for d in (1, 2, 3)]
    peers += [
        {"leaf": partner, "front": lax.rem(y + d, 4) * 4 + x} for d in (0, 1, 2, 3)
    ]
    for peer in peers:
        pl.semaphore_signal(barrier, inc=1, device_id=peer, device_id_type=MESH)

    def lanes(t):
        return pl.ds(pl.multiple_of(t * 128, 128), 128)

    def tiles(p):
        return lanes(p + lax.div(p + 1, 2)), lanes(1 + 3 * lax.div(p, 2))

    full_tile, half_tile = tiles(x)
    moves = [
        (idx_in.at[pl.ds(pl.multiple_of(lax.div(leaf, 4) * 8, 8), 8), :], idx_s),
        (owner_in, owner),
        (e_in.at[:, :, lanes(x)], e_s.at[:, pl.ds(y * 128 + x * 32, 32), :]),
        (d_in.at[:, full_tile], dp_s.at[0, pl.ds(x * 48, 48), :]),
        (d_in.at[:, half_tile], dp_s.at[1, pl.ds(x * 48, 48), :]),
        (cf_in, cf_s.at[:, pl.ds(x * 64, 64), :]),
        (d_in, d_s.at[pl.ds(x * 48, 48), :]),
        (f_in, f_s.at[pl.ds(x * 96, 96), :]),
        (b_in, b_s.at[pl.ds(x * 96, 96), :]),
    ]
    moves = [pltpu.make_async_copy(src, dst, loc.at[i]) for i, (src, dst) in enumerate(moves)]
    own_idx, own_owner, own_e, own_dp0, own_dp1, own_cf, own_d, own_f, own_b = moves
    for copy in moves:
        copy.start()

    e_across, d_across = [], []
    for d in (1, 3, 2):
        other = lax.rem(x + d, 4)
        e_across.append(remote(
            e_in.at[:, :, lanes(other)], e_s.at[:, pl.ds(y * 128 + x * 32, 32), :], at_x(other)
        ))
    for d in (1, 3, 2):
        other = lax.rem(x + d, 4)
        for t, tile in enumerate(tiles(other)):
            d_across.append(remote(
                d_in.at[:, tile], dp_s.at[t, pl.ds(x * 48, 48), :], at_x(other)
            ))
    ring_cf = Ring(at_x, x, lambda p, h: cf_s.at[h, pl.ds(p * 64, 64), :], lambda h: cf_in.at[h])
    ring_d = Ring(at_x, x, halves(d_s, 48), of(d_in, 48))
    ring_f = Ring(at_x, x, halves(f_s, 96), of(f_in, 96))
    ring_b = Ring(at_x, x, halves(b_s, 96), of(b_in, 96))
    ring_e = Ring(at_y, y, lambda p, h: e_s.at[h, pl.ds(p * 128, 128), :])
    ring_dp = Ring(at_y, y, halves(v_s, 192, 0))
    ring_dh = Ring(at_y, y, halves(v_pack, 96))
    ring_k = [Ring(at_y, y, halves(k_s, 256, c)) for c in range(2)]
    ring_v = [Ring(at_y, y, halves(v_s, 192, 1 + c)) for c in range(2)]
    ring_w = Ring(at_y, y, halves(r_s, 384, 0))
    ring_wh = Ring(at_y, y, halves(w_pack, 192))
    ring_r = [Ring(at_y, y, halves(r_s, 384, 1 + c)) for c in range(2)]
    k_cross = remote(k_own, k_par, {"leaf": partner})

    pl.semaphore_wait(barrier, 10)

    for copy in e_across + d_across:
        copy.start()
    ring_cf.begin()

    own_owner.wait()
    own_idx.wait()
    pool = (2 * leaf, 2 * leaf + 1, 2 * partner, 2 * partner + 1)
    mine = [(owner[p] == leaf).astype(jnp.int32) for p in pool]
    in_eight = [lax.rem(p, 8) for p in pool]

    def pick(c, items):
        if c == 0:
            return select(mine[0], items[0], select(mine[1], items[1], items[2]))
        return select(mine[3], items[3], select(mine[2], items[2], items[1]))

    idx_rows = [idx_s[pl.ds(p, 1), :] for p in in_eight]

    def one_hot(c):
        positions = pick(c, idx_rows)
        for m in range(0, 768, 128):
            at = lax.broadcasted_iota(jnp.int32, (128, 1024), 0) + m
            su[c, pl.ds(m, 128), :] = jnp.where(at == positions, 1.0, 0.0).astype(BF16)
        for m in range(0, 384, 128):
            at = lax.broadcasted_iota(jnp.int32, (128, 1024), 0) + (768 + 384 * y + m)
            sl[c, pl.ds(m, 128), :] = jnp.where(at == positions, 1.0, 0.0).astype(BF16)

    def split_rows(src, hi, lo, size, step):
        for m in range(0, size, step):
            h, l = split(src[pl.ds(m, step), :])
            hi[pl.ds(m, step), :] = h
            lo[pl.ds(m, step), :] = l

    def low_lanes(shape):
        return lax.broadcasted_iota(jnp.int32, shape, 1) < 64

    def pack(top, bottom):
        return jnp.where(low_lanes(top.shape), top, pltpu.roll(bottom, 64, 1))

    own_e.wait()
    for copy in e_across:
        copy.wait_recv()
    ring_e.begin()
    one_hot(0)

    own_dp0.wait()
    own_dp1.wait()
    for copy in d_across:
        copy.wait_recv()
    whole = dp_s[0]
    half = dp_s[1]
    half = select(lax.rem(x, 2), pltpu.roll(half, 64, 1), half)
    d_sums = [col_sum(whole * whole), col_sum(half * half)]
    v_s[0, pl.ds(pl.multiple_of(y * 192, 192), 192), :] = whole
    v_pack[pl.ds(pl.multiple_of(y * 96, 96), 96), :] = pack(half[:96], half[96:])
    ring_dp.begin()
    ring_dh.begin()
    ring_e.relay()
    ring_cf.relay()
    ring_d.begin()
    one_hot(1)
    ring_dp.relay()
    ring_dh.relay()

    ring_e.finish()
    e_sums = []
    for c in range(2):
        for m in range(0, 512, 128):
            h, l = split(e_s[c, pl.ds(m, 128), :])
            eh[c, pl.ds(m, 128), :] = h
            el[c, pl.ds(m, 128), :] = l
        part = e_s[c, pl.ds(pl.multiple_of(y * 128, 128), 128), :]
        e_sums.append(col_sum(part * part))
    own_cf.wait()
    ring_cf.finish()
    for c in range(2):
        for m in range(0, 256, 64):
            h, l = split(cf_s[c, pl.ds(m, 64), :])
            ch[c, pl.ds(m, 64), :] = h
            cl[c, pl.ds(m, 64), :] = l
        for m in range(0, 256, 128):
            at = pl.ds(m, 128)
            k_own[c, at, :] = dot3(ch[c, at, :], cl[c, at, :], eh[c], el[c])
    k_cross.start()
    ring_d.relay()
    ring_f.begin()
    k_cross.wait_recv()
    for c in range(2):
        for m in range(0, 256, 64):
            at = pl.ds(m, 64)
            pooled = [k_own[0, at, :], k_own[1, at, :], k_par[0, at, :], k_par[1, at, :]]
            k_s[c, pl.ds(pl.multiple_of(y * 256 + m, 64), 64), :] = pick(c, pooled)
        ring_k[c].begin()

    def split_to(value, hi, lo, row, col):
        h, l = split(value)
        hi[row, pl.ds(col, 128)] = h
        lo[row, pl.ds(col, 128)] = l

    ring_dp.finish()
    ring_dh.finish()
    for p in range(4):
        for m in (0, 96):
            split_to(v_s[0, pl.ds(192 * p + m, 96), :], vh, vl, pl.ds(192 * p + m, 96), 0)
            value = v_pack[pl.ds(96 * p, 96), :]
            if m:
                value = pltpu.roll(value, 64, 1)
            split_to(value, vh, vl, pl.ds(192 * p + m, 96), 128)
    ring_k[0].relay()
    own_d.wait()
    ring_d.finish()
    split_rows(d_s, dh, dl, 192, 48)
    ring_k[1].relay()
    ring_f.relay()
    ring_b.begin()

    v_sums = []
    for c in range(2):
        ring_k[c].finish()
        for m in range(0, 1024, 128):
            h, l = split(k_s[c, pl.ds(m, 128), :])
            kh[c, pl.ds(m, 128), :] = h
            kl[c, pl.ds(m, 128), :] = l
        for m in range(0, 768, 256):
            at = pl.ds(m, 256)
            uh[at, pl.ds(c * 128, 128)] = dot(su[c, at, :], kh[c]).astype(BF16)
            ul[at, pl.ds(c * 128, 128)] = dot(su[c, at, :], kl[c]).astype(BF16)
        cols = pl.ds(c * 128, 128)
        value = dot3(dh[...], dl[...], uh[:, cols], ul[:, cols])
        v_s[1 + c, pl.ds(pl.multiple_of(y * 192, 192), 192), :] = value
        v_sums.append(col_sum(value * value))
        ring_v[c].begin()

    ring_v[0].relay()
    own_f.wait()
    ring_f.finish()
    split_rows(f_s, fh, fl, 384, 48)
    ring_v[1].relay()
    parts = []
    for m in (0, 192):
        at = pl.ds(m, 192)
        value = dot3(fh[at, :], fl[at, :], vh[...], vl[...])
        r_s[0, pl.ds(pl.multiple_of(y * 384 + m, 192), 192), :] = value[:, :128]
        w_half[at, :] = value[:, 128:]
    ring_w.begin()
    w_pack[pl.ds(pl.multiple_of(y * 192, 192), 192), :] = pack(w_half[0:192, :], w_half[192:384, :])
    for c in range(2):
        for m in range(0, 384, 128):
            at = pl.ds(m, 128)
            l_s[at, pl.ds(c * 128, 128)] = dot(sl[c, at, :], kh[c]) + dot(sl[c, at, :], kl[c])

    for c in range(2):
        ring_v[c].finish()
        cols = pl.ds(c * 128, 128)
        for m in range(0, 768, 128):
            split_to(v_s[1 + c, pl.ds(m, 128), :], vh, vl, pl.ds(m, 128), 128 * c)
        for m in (0, 192):
            at = pl.ds(m, 192)
            value = l_s[at, cols] - dot3(fh[at, :], fl[at, :], vh[:, cols], vl[:, cols])
            r_s[1 + c, pl.ds(pl.multiple_of(y * 384 + m, 192), 192), :] = value
        ring_r[c].begin()
        if c == 0:
            ring_w.relay()
    ring_b.relay()
    ring_r[0].relay()
    ring_wh.begin()
    ring_w.finish()
    own_b.wait()
    ring_b.finish()
    split_rows(b_s, bh, bl, 384, 24)
    ring_r[1].relay()
    ring_wh.relay()

    ring_r[0].finish()
    for t in range(2):
        for m in range(0, 1536, 128):
            split_to(r_s[t, pl.ds(m, 128), :], rh, rl, pl.ds(m, 128), 128 * t)
    sums = [jnp.zeros((1, 128), F32)] * 4
    for m in range(0, 384, 128):
        at = pl.ds(m, 128)
        value = dot3(bh[at, :], bl[at, :], rh[...], rl[...])
        to = pl.ds(pl.multiple_of(y * 384 + m, 128), 128)
        for t in range(2):
            sums[t] = sums[t] + col_sum(value[:, t * 128:(t + 1) * 128] * r_s[t, to, :])

    def add_rows(p, first):
        for h in range(2):
            row = pl.ds(pl.multiple_of(p * 384 + h * 192, 192), 192)
            value = w_pack[pl.ds(pl.multiple_of(p * 192, 192), 192), :]
            if h:
                value = pltpu.roll(value, 64, 1)
            split_to(value, rh, rl, row, 0)
            split_to(r_s[2, row, :], rh, rl, row, 128)
        cols = pl.ds(pl.multiple_of(p * 384, 128), 384)
        row = pl.ds(pl.multiple_of(p * 384, 384), 384)
        for m in range(0, 384, 128):
            at = pl.ds(m, 128)
            value = dot3(bh[at, cols], bl[at, cols], rh[row, :], rl[row, :])
            acc[at, :] = value if first else acc[at, :] + value

    ring_wh.finish()
    add_rows(y, True)
    ring_r[1].near()
    add_rows(lax.rem(y + 1, 4), False)
    add_rows(lax.rem(y + 3, 4), False)
    ring_r[1].far()
    add_rows(lax.rem(y + 2, 4), False)
    for m in range(0, 384, 128):
        at = pl.ds(m, 128)
        to = pl.ds(pl.multiple_of(y * 384 + m, 128), 128)
        sums[2] = sums[2] + col_sum(acc[at, 0:128] * w_half[at, :])
        sums[3] = sums[3] + col_sum(acc[at, 128:256] * r_s[2, to, :])

    stage[0:1, :] = sums[0] + d_sums[0]
    stage[1:2, :] = sums[2] + d_sums[1]
    stage[2:3, :] = sums[1] + v_sums[0]
    stage[3:4, :] = sums[3] + v_sums[1]
    stage[4:5, :] = e_sums[0]
    stage[5:6, :] = e_sums[1]
    stage[6:8, :] = jnp.zeros((2, 128), F32)
    fin[0, y] = stage[...]
    ends = []
    for d in (1, 3, 2):
        ends.append(remote(stage, fin.at[0, y], at_y(lax.rem(y + d, 4))))
    for d in (0, 1, 3, 2):
        ends.append(remote(stage, fin.at[1, y], {"leaf": partner, "front": lax.rem(y + d, 4) * 4 + x}))
    for copy in ends:
        copy.start()
    for copy in ends:
        copy.wait_recv()
    own = ((fin[0, 0] + fin[0, 1]) + fin[0, 2]) + fin[0, 3]
    other = ((fin[1, 0] + fin[1, 1]) + fin[1, 2]) + fin[1, 3]
    before = 2 - mine[2] - mine[3]
    quad_0 = select(mine[0], own[2:3], select(before, other[3:4], other[2:3]))
    quad_1 = select(mine[1], select(mine[0], own[3:4], own[2:3]), other[3:4])
    ostage[0:2, :] = own[0:2]
    ostage[2:3, :] = own[4:5] + quad_0
    ostage[3:4, :] = own[5:6] + quad_1
    ostage[4:8, :] = jnp.zeros((4, 128), F32)
    xfin[x] = ostage[...]
    ends = []
    for d in (1, 3, 2):
        ends.append(remote(ostage, xfin.at[x], at_x(lax.rem(x + d, 4))))
    for copy in ends:
        copy.start()
    for copy in ends:
        copy.wait_recv()
    for p, t in enumerate((0, 2, 3, 5)):
        out[t:t + 1, :] = xfin[p, 0:1, :]
        out[8 + 2 * p:10 + 2 * p, :] = xfin[p, 2:4, :]
    for p, t in ((0, 1), (2, 4)):
        out[t:t + 1, :] = pack(xfin[p, 1:2, :], xfin[p + 1, 1:2, :])
    out[6:8, :] = jnp.zeros((2, 128), F32)
    for copy in copies:
        copy.wait_send()


COPIES = 110


def shards(b, f, d, cf, e, idx, owner):
    vm = pltpu.VMEM
    any_spec = pl.BlockSpec(memory_space=pl.ANY)
    vmem_spec = pl.BlockSpec(memory_space=pltpu.VMEM)
    out = pl.pallas_call(
        kernel,
        out_shape=jax.ShapeDtypeStruct((16, 128), F32),
        in_specs=[any_spec] * 7,
        out_specs=vmem_spec,
        scratch_shapes=[
            vm((384, 1536), F32), vm((384, 768), F32), vm((192, 768), F32),
            vm((2, 256, 512), F32), vm((2, 512, 128), F32), vm((2, 192, 128), F32),
            vm((2, 256, 128), F32), vm((2, 256, 128), F32), vm((2, 1024, 128), F32),
            vm((3, 768, 128), F32), vm((384, 128), F32),
            vm((3, 1536, 128), F32), vm((384, 128), F32), vm((768, 128), F32),
            vm((8, 1024), jnp.int32), vm((384, 256), F32), vm((384, 256), F32),
            pltpu.SMEM((64,), jnp.int32),
            vm((2, 768, 1024), BF16), vm((2, 384, 1024), BF16),
            vm((384, 1536), BF16), vm((384, 1536), BF16),
            vm((384, 768), BF16), vm((384, 768), BF16),
            vm((192, 768), BF16), vm((192, 768), BF16),
            vm((2, 256, 512), BF16), vm((2, 256, 512), BF16),
            vm((2, 512, 128), BF16), vm((2, 512, 128), BF16),
            vm((2, 1024, 128), BF16), vm((2, 1024, 128), BF16),
            vm((768, 256), BF16), vm((768, 256), BF16),
            vm((768, 256), BF16), vm((768, 256), BF16),
            vm((1536, 256), BF16), vm((1536, 256), BF16),
            vm((8, 128), F32), vm((2, 4, 8, 128), F32), vm((8, 128), F32), vm((4, 8, 128), F32),
            pltpu.SemaphoreType.DMA((COPIES,)),
            pltpu.SemaphoreType.DMA((COPIES,)),
            pltpu.SemaphoreType.DMA((9,)),
        ],
        compiler_params=pltpu.CompilerParams(
            collective_id=0, has_side_effects=True, vmem_limit_bytes=60 * 1024 * 1024
        ),
        name="selected",
    )(b[0], f[0], d[0], cf, e, idx, owner)
    kids = out[8:16].reshape(4, 2, 128).transpose(1, 0, 2).reshape(2, 512)
    return out[0:6].reshape(1, 768), kids


def solution(mesh):
    split_spec = P("leaf", "front", None)
    in_specs = (split_spec,) * 5 + (P(), P())
    out_specs = (P("leaf", None), P("leaf", None))
    return jax.shard_map(shards, mesh=mesh, in_specs=in_specs, out_specs=out_specs, check_vma=False)
```

time: 88.7 us -> 83.3 us (0.939)
  Pallas kernels: 86 us -> 80.6 us
    pallas_call x1, Pallas kernels: 86 us -> 80.6 us  [shards(): pl.pallas_call(kernel, out_shape=jax.ShapeDtypeStruct((16, 128), F32), in...]
    unnamed x6 -> x4, local copies, waits for them, and re-layouts: 1.83 us -> 1.32 us
where the time goes in v2:
time: 83.3 us; the launch traced here: 83.1 us
  Pallas kernels  80.6 us (97%)
  local copies, waits for them, and re-layouts  1.92 us (2%)
    pallas_call x1, Pallas kernels, shards(): pl.pallas_call(kernel, out_shape=jax.ShapeDtypeStruct((16, 128), F32), in...  80.6 us

profile of v2, /device:TPU:1, one launch (start us, length us, event | category | flops | bytes accessed | tf_op | source)
XLA Modules:
  0.0 83.1 jit_solution(8677896314729120316)
XLA Ops:
  0.6 80.6 %selected.1 = f32[16,128]{1,0:T(8,128)} custom-call(f32[96,1536]{1,0:T(8,128)} %bitcast.14, f32[96,768]{1,0:T(8,128)} %bitcast.15, f32[48,768]{1,0:T(8,128)} %bitcast.16, f32[2,64,512]{2,1,0:T(8,128)} %cf_in.1, f32[2,32,512]{2,1,0:T(8,128)} %e_in.1, s32[64,1024]{1,0:T(8,128)} %idx_in.1, s32[64]{0:T(128)} %owner_in.1), custom_call_target="tpu_custom_call" | custom-call | tf_op jit(solution)/shard_map/selected/pallas_call | solution.py:425
  81.2 0.0 copy-start
  81.2 0.7 slice_bitcast_fusion
  81.9 0.6 copy.12
  82.5 0.0 copy-done
  82.5 0.6 slice.7
Async XLA Ops:
  81.2 1.3 %copy-start = (f32[16,128]{1,0:T(8,128)S(1)}, f32[16,128]{1,0:T(8,128)}, u32[]{:S(2)}) copy-start(f32[16,128]{1,0:T(8,128)} %selected.1) | copy-start | bytes 24580

commit v3 on v2

v3 whole, which is shorter than its diff:
```python
import jax
import jax.numpy as jnp
from jax import lax
from jax.experimental import pallas as pl
from jax.experimental.pallas import tpu as pltpu
from jax.sharding import PartitionSpec as P

F32 = jnp.float32
BF16 = jnp.bfloat16
MESH = pl.DeviceIdType.MESH


def dot(a, b):
    return jnp.dot(a, b, preferred_element_type=F32)


def dot3(ah, al, bh, bl):
    return dot(ah, bh) + (dot(ah, bl) + dot(al, bh))


def split(x):
    hi = x.astype(BF16)
    return hi, (x - hi.astype(F32)).astype(BF16)


def col_sum(x):
    return jnp.sum(x, axis=0, keepdims=True)


def select(flag, yes, no):
    return jnp.where(jnp.full(yes.shape, flag, jnp.int32) == 1, yes, no)


def kernel(
    b_in, f_in, d_in, cf_in, e_in, idx_in, owner_in,
    out,
    e_raw, c_raw, e_sel, c_sel,
    b_s, f_s, d_s, cf_s, e_s, dp_s, k_s, v_s, v_pack, r_s, w_half, w_pack, w_tile, w_side,
    idx_s, l_s, acc, owner,
    su, sl, bh, bl, fh, fl, dh, dl, ch, cl, eh, el, kh, kl, uh, ul, vh, vl, wh, wl, rh, rl,
    stage, fin, ostage, xfin, send, recv, loc,
):
    leaf = lax.axis_index("leaf")
    front = lax.axis_index("front")
    y = lax.div(front, 4)
    x = lax.rem(front, 4)
    core = lax.rem(leaf, 2)
    base = leaf - core
    partner = base + 1 - core
    group = lax.div(x, 2)
    pair = x + 1 - 2 * lax.rem(x, 2)
    col = 2 * lax.rem(x, 2) + core
    hub = core == group
    copies, hub_copies, kept_copies = [], [], []
    taken = [0, 0]

    def remote(src, dst, device, group_of=None, at=None):
        if at is None:
            at = taken[1]
            taken[1] += 1
        copy = pltpu.make_async_remote_copy(
            src_ref=src, dst_ref=dst, send_sem=send.at[taken[0]], recv_sem=recv.at[at],
            device_id=device, device_id_type=MESH,
        )
        taken[0] += 1
        (copies if group_of is None else group_of).append(copy)
        return copy

    def slots(n):
        taken[1] += n
        return taken[1] - n

    def at_y(p):
        return {"front": p * 4 + x}

    def on(chip, a_core=None):
        if a_core is None:
            return {"front": y * 4 + chip}
        return {"leaf": base + a_core, "front": y * 4 + chip}

    other_core = {"leaf": partner}

    class Ring:
        def __init__(self, part):
            right, left = lax.rem(y + 1, 4), lax.rem(y + 3, 4)
            self.right = [remote(part(y, h), part(y, h), at_y(right)) for h in (0, 1)]
            self.left = [remote(part(y, h), part(y, h), at_y(left)) for h in (1, 0)]
            self.next_right = remote(part(left, 0), part(left, 0), at_y(right))
            self.next_left = remote(part(right, 1), part(right, 1), at_y(left))

        def begin(self):
            for h in range(2):
                self.right[h].start()
                self.left[h].start()

        def relay(self):
            self.right[0].wait_recv()
            self.next_right.start()
            self.left[0].wait_recv()
            self.next_left.start()

        def near(self):
            self.right[1].wait_recv()
            self.left[1].wait_recv()

        def far(self):
            self.next_right.wait_recv()
            self.next_left.wait_recv()

        def finish(self):
            self.near()
            self.far()

    class Rows:
        def __init__(self, part, whole, src, local):
            first = slots(4)
            role = jnp.where(hub, 0, 2)
            goal = jnp.where(hub, pair, 3 - x)
            self.first = [remote(src(h), part(x, h), on(goal), at=first + role + h) for h in (0, 1)]
            self.pair_in = [
                pltpu.make_async_remote_copy(
                    src_ref=part(pair, h), dst_ref=part(pair, h), send_sem=send.at[0],
                    recv_sem=recv.at[first + h], device_id=on(pair), device_id_type=MESH,
                ) for h in (0, 1)
            ]
            self.far_in = [
                pltpu.make_async_remote_copy(
                    src_ref=part(3 - x, h), dst_ref=part(3 - x, h), send_sem=send.at[0],
                    recv_sem=recv.at[first + 2 + h], device_id=on(pair), device_id_type=MESH,
                ) for h in (0, 1)
            ]
            self.next = [
                remote(part(3 - x, h), part(3 - x, h), on(pair), hub_copies) for h in (0, 1)
            ]
            self.inside = [
                remote(whole(p), whole(p), other_core, hub_copies) for p in (x, 3 - x, pair, 3 - pair)
            ]
            self.own, self.whole = local, whole

        def keep(self, sem):
            self.local = pltpu.make_async_copy(self.own, self.whole(x), loc.at[sem])

            @pl.when(hub)
            def _():
                self.local.start()

        def begin(self):
            for h in range(2):
                self.first[h].start()

        def relay(self):
            @pl.when(hub)
            def _():
                self.local.wait()
                self.inside[0].start()
                for h in range(2):
                    self.far_in[h].wait_recv()
                    self.next[h].start()
                self.inside[1].start()

        def near(self):
            @pl.when(hub)
            def _():
                for h in range(2):
                    self.pair_in[h].wait_recv()
                self.inside[2].start()

        def finish(self):
            @pl.when(hub)
            def _():
                for h in range(2):
                    self.next[h].wait_recv()
                self.inside[3].start()

            @pl.when(jnp.logical_not(hub))
            def _():
                for copy in self.inside:
                    copy.wait_recv()

    def halves(ref, size, *lead):
        return lambda p, h: ref.at[(*lead, pl.ds(p * size + h * (size // 2), size // 2), slice(None))]

    def wholes(ref, size):
        return lambda p: ref.at[pl.ds(p * size, size), :]

    def of(ref, size):
        return lambda h: ref.at[pl.ds(h * (size // 2), size // 2), :]

    barrier = pltpu.get_barrier_semaphore()
    peers = [at_y(lax.rem(y + d, 4)) for d in (1, 2, 3)]
    row_peers = [on(lax.rem(x + d, 4), core) for d in (1, 3, 2)]
    row_peers += [on(lax.rem(x + d, 4), 1 - core) for d in (0, 1, 3, 2)]
    for peer in peers + row_peers:
        pl.semaphore_signal(barrier, inc=1, device_id=peer, device_id_type=MESH)

    def lanes(t):
        return pl.ds(pl.multiple_of(t * 128, 128), 128)

    def tiles(p):
        return lanes(p + lax.div(p + 1, 2)), lanes(1 + 3 * lax.div(p, 2))

    full_tile, half_tile = tiles(col)
    moves = [
        (idx_in.at[pl.ds(pl.multiple_of(lax.div(leaf, 4) * 8, 8), 8), :], idx_s),
        (owner_in, owner),
        (e_in, e_raw.at[0]),
        (cf_in, c_raw.at[0]),
    ]
    moves = [pltpu.make_async_copy(src, dst, loc.at[i]) for i, (src, dst) in enumerate(moves)]
    own_idx, own_owner, own_e, own_cf = moves
    for copy in (own_owner, own_e, own_cf, own_idx):
        copy.start()

    e_cross = remote(e_in, e_raw.at[1], other_core)
    c_cross = remote(cf_in, c_raw.at[1], other_core)

    e_rows = lambda p: e_s.at[:, pl.ds(y * 128 + p * 32, 32), :]
    d_rows = lambda t, p: dp_s.at[t, pl.ds(p * 48, 48), :]
    e_at, d_at = slots(4), slots(8)
    e_across, d_across, is_own = [], [], []
    for j in range(4):
        goal = on(2 * core + j // 2, j % 2)
        is_own.append(jnp.logical_and(hub, col == j))
        e_across.append([remote(e_sel.at[:, :, lanes(j)], e_rows(x), goal, kept_copies, e_at + x)])
        d_across.append([
            remote(d_in.at[:, tile], d_rows(t, x), goal, kept_copies, d_at + 2 * x + t)
            for t, tile in enumerate(tiles(jnp.int32(j)))
        ])

    def arriving(dst, at):
        return pltpu.make_async_remote_copy(
            src_ref=dst, dst_ref=dst, send_sem=send.at[0], recv_sem=recv.at[at],
            device_id=on(pair), device_id_type=MESH,
        )

    e_kept = [pltpu.make_async_copy(e_sel.at[:, :, lanes(col)], e_rows(x), loc.at[4])]
    d_kept = [
        pltpu.make_async_copy(d_in.at[:, full_tile], d_rows(0, x), loc.at[5]),
        pltpu.make_async_copy(d_in.at[:, half_tile], d_rows(1, x), loc.at[6]),
    ]

    def scatter(across, kept):
        @pl.when(hub)
        def _():
            for copy in kept:
                copy.start()

        for j in range(4):
            @pl.when(jnp.logical_not(is_own[j]))
            def _(j=j):
                for copy in across[j]:
                    copy.start()

    def gather(kept, pieces):
        @pl.when(hub)
        def _():
            for copy in kept:
                copy.wait()

        for p in range(4):
            @pl.when(jnp.logical_not(jnp.logical_and(hub, x == p)))
            def _(p=p):
                for copy in pieces(p):
                    copy.wait_recv()

    rows_c = Rows(
        lambda p, h: cf_s.at[h, pl.ds(p * 64, 64), :], lambda p: cf_s.at[:, pl.ds(p * 64, 64), :],
        lambda h: c_sel.at[h], c_sel,
    )
    rows_f = Rows(halves(f_s, 96), wholes(f_s, 96), of(f_in, 96), f_in)
    rows_d = Rows(halves(d_s, 48), wholes(d_s, 48), of(d_in, 48), d_in)
    rows_b = Rows(halves(b_s, 96), wholes(b_s, 96), of(b_in, 96), b_in)
    ring_e = Ring(lambda p, h: e_s.at[h, pl.ds(p * 128, 128), :])
    ring_dp = Ring(halves(v_s, 192))
    ring_dh = Ring(halves(v_pack, 96))
    ring_k = [Ring(halves(k_s, 256, c)) for c in range(2)]
    ring_w = Ring(halves(r_s, 384, 0))
    ring_wh = Ring(halves(w_pack, 192))
    ring_r = [Ring(halves(r_s, 384, 1 + c)) for c in range(2)]
    w_pair, w_in, w_on = [], [], []
    for ref in (w_tile, w_side):
        w_pair.append(remote(ref.at[col], ref.at[col], on(pair)))
        w_in.append(remote(ref.at[col], ref.at[col], other_core))
    for ref in (w_tile, w_side):
        far_col = 2 * lax.rem(pair, 2) + core
        w_on.append(remote(ref.at[far_col], ref.at[far_col], other_core))

    rows_f.keep(7)
    rows_d.keep(8)
    rows_b.keep(9)

    pl.semaphore_wait(barrier, 10)

    e_cross.start()
    c_cross.start()
    scatter(d_across, d_kept)

    def members(mine_leaf, other_leaf):
        pool = (2 * mine_leaf, 2 * mine_leaf + 1, 2 * other_leaf, 2 * other_leaf + 1)
        return pool, [(owner[p] == mine_leaf).astype(jnp.int32) for p in pool]

    def pick(c, flags, items):
        if c == 0:
            return select(flags[0], items[0], select(flags[1], items[1], items[2]))
        return select(flags[3], items[3], select(flags[2], items[2], items[1]))

    own_owner.wait()
    _, mine = members(leaf, partner)
    pool, held = members(base + group, base + 1 - group)
    own_e.wait()
    e_cross.wait_recv()
    for c in range(2):
        e_sel[c] = pick(c, mine, [e_raw[0, 0], e_raw[0, 1], e_raw[1, 0], e_raw[1, 1]])
    scatter(e_across, e_kept)
    own_cf.wait()
    c_cross.wait_recv()
    for c in range(2):
        for m in (0, 32):
            at = pl.ds(m, 32)
            c_sel[c, at, :] = pick(
                c, mine, [c_raw[0, 0, at, :], c_raw[0, 1, at, :], c_raw[1, 0, at, :], c_raw[1, 1, at, :]]
            )
    rows_c.begin()
    rows_c.keep(10)

    own_idx.wait()
    idx_rows = [idx_s[pl.ds(lax.rem(p, 8), 1), :] for p in pool]

    def one_hot(c):
        positions = pick(c, held, idx_rows)
        for m in range(0, 768, 128):
            at = lax.broadcasted_iota(jnp.int32, (128, 1024), 0) + m
            su[c, pl.ds(m, 128), :] = jnp.where(at == positions, 1.0, 0.0).astype(BF16)
        for m in range(0, 384, 128):
            at = lax.broadcasted_iota(jnp.int32, (128, 1024), 0) + (768 + 384 * y + m)
            sl[c, pl.ds(m, 128), :] = jnp.where(at == positions, 1.0, 0.0).astype(BF16)

    def split_rows(src, hi, lo, size, step):
        for m in range(0, size, step):
            h, l = split(src[pl.ds(m, step), :])
            hi[pl.ds(m, step), :] = h
            lo[pl.ds(m, step), :] = l

    def split_to(value, hi, lo, row, lane):
        h, l = split(value)
        hi[row, pl.ds(lane, 128)] = h
        lo[row, pl.ds(lane, 128)] = l

    def low_lanes(shape):
        return lax.broadcasted_iota(jnp.int32, shape, 1) < 64

    def swap(value):
        return pltpu.roll(value, 64, 1)

    def pack(top, bottom):
        return jnp.where(low_lanes(top.shape), top, swap(bottom))

    gather(d_kept, lambda p: [arriving(d_rows(t, p), d_at + 2 * p + t) for t in range(2)])
    whole = dp_s[0]
    half = select(core, swap(dp_s[1]), dp_s[1])
    d_sums = [col_sum(whole * whole), col_sum(half * half)]
    v_s[pl.ds(pl.multiple_of(y * 192, 192), 192), :] = whole
    v_pack[pl.ds(pl.multiple_of(y * 96, 96), 96), :] = pack(half[:96], half[96:])
    ring_dp.begin()
    ring_dh.begin()
    gather(e_kept, lambda p: [arriving(e_rows(p), e_at + p)])
    ring_e.begin()
    rows_c.relay()
    rows_f.begin()
    one_hot(0)
    ring_dp.relay()
    ring_dh.relay()
    rows_c.near()
    ring_e.relay()

    ring_e.finish()
    e_sums = []
    for c in range(2):
        for m in range(0, 512, 128):
            h, l = split(e_s[c, pl.ds(m, 128), :])
            eh[c, pl.ds(m, 128), :] = h
            el[c, pl.ds(m, 128), :] = l
        part = e_s[c, pl.ds(pl.multiple_of(y * 128, 128), 128), :]
        e_sums.append(col_sum(part * part))
    rows_c.finish()
    for c in range(2):
        for m in range(0, 256, 64):
            h, l = split(cf_s[c, pl.ds(m, 64), :])
            ch[c, pl.ds(m, 64), :] = h
            cl[c, pl.ds(m, 64), :] = l
        for m in range(0, 256, 128):
            at = pl.ds(m, 128)
            k_s[c, pl.ds(pl.multiple_of(y * 256 + m, 128), 128), :] = dot3(ch[c, at, :], cl[c, at, :], eh[c], el[c])
        ring_k[c].begin()
    rows_f.relay()
    rows_d.begin()
    one_hot(1)
    rows_f.near()

    ring_dp.finish()
    ring_dh.finish()
    for p in range(4):
        for m in (0, 96):
            split_to(v_s[pl.ds(192 * p + m, 96), :], vh, vl, pl.ds(192 * p + m, 96), 0)
            value = v_pack[pl.ds(96 * p, 96), :]
            split_to(swap(value) if m else value, vh, vl, pl.ds(192 * p + m, 96), 128)
    ring_k[0].relay()
    rows_f.finish()
    split_rows(f_s, fh, fl, 384, 48)
    for m in (0, 192):
        at = pl.ds(m, 192)
        value = dot3(fh[at, :], fl[at, :], vh[...], vl[...])
        r_s[0, pl.ds(pl.multiple_of(y * 384 + m, 192), 192), :] = value[:, :128]
        w_tile[col, at, :] = value[:, :128]
        w_half[at, :] = value[:, 128:]
    packed = pack(w_half[0:192, :], w_half[192:384, :])
    w_pack[pl.ds(pl.multiple_of(y * 192, 192), 192), :] = packed
    w_side[col] = packed
    for copy in w_pair + w_in:
        copy.start()
    ring_k[1].relay()
    ring_w.begin()
    rows_d.relay()
    rows_b.begin()
    rows_d.near()

    for c in range(2):
        ring_k[c].finish()
        for m in range(0, 1024, 128):
            h, l = split(k_s[c, pl.ds(m, 128), :])
            kh[c, pl.ds(m, 128), :] = h
            kl[c, pl.ds(m, 128), :] = l
        for m in range(0, 768, 256):
            at = pl.ds(m, 256)
            uh[at, pl.ds(c * 128, 128)] = dot(su[c, at, :], kh[c]).astype(BF16)
            ul[at, pl.ds(c * 128, 128)] = dot(su[c, at, :], kl[c]).astype(BF16)
        if c == 0:
            ring_w.relay()
            ring_wh.begin()
        for m in range(0, 384, 128):
            at = pl.ds(m, 128)
            l_s[at, pl.ds(c * 128, 128)] = dot(sl[c, at, :], kh[c]) + dot(sl[c, at, :], kl[c])

    for copy in w_pair:
        copy.wait_recv()
    for copy in w_on:
        copy.start()
    rows_d.finish()
    for copy in w_in + w_on:
        copy.wait_recv()
    for p, t in enumerate((0, 2, 3, 5)):
        for m in (0, 192):
            split_to(w_tile[p, pl.ds(m, 192), :], wh, wl, pl.ds(m, 192), 128 * t)
    for p, t in ((0, 1), (2, 4)):
        low, high = w_side[p], w_side[p + 1]
        split_to(jnp.where(low_lanes(low.shape), low, swap(high)), wh, wl, pl.ds(0, 192), 128 * t)
        split_to(jnp.where(low_lanes(low.shape), swap(low), high), wh, wl, pl.ds(192, 192), 128 * t)
    for c in range(2):
        cols = pl.ds(c * 128, 128)
        for m in (0, 192):
            at = pl.ds(m, 192)
            value = l_s[at, cols] - dot3(wh[at, :], wl[at, :], uh[:, cols], ul[:, cols])
            r_s[1 + c, pl.ds(pl.multiple_of(y * 384 + m, 192), 192), :] = value
        ring_r[c].begin()
    ring_wh.relay()
    rows_b.relay()
    rows_b.near()
    split_rows(d_s, dh, dl, 192, 48)
    value = dot3(dh[...], dl[...], uh[...], ul[...])
    v_sums = col_sum(value * value)
    ring_r[0].relay()
    ring_r[1].relay()
    ring_w.finish()
    ring_wh.finish()
    rows_b.finish()
    split_rows(b_s, bh, bl, 384, 24)

    def split_half(p):
        value = w_pack[pl.ds(pl.multiple_of(p * 192, 192), 192), :]
        split_to(value, rh, rl, pl.ds(pl.multiple_of(p * 384, 192), 192), 128)
        split_to(swap(value), rh, rl, pl.ds(pl.multiple_of(p * 384 + 192, 192), 192), 128)

    for p in range(4):
        split_half(p)
    for m in range(0, 1536, 128):
        split_to(r_s[0, pl.ds(m, 128), :], rh, rl, pl.ds(m, 128), 0)
    p_sums = list(d_sums)
    for m in range(0, 384, 128):
        at = pl.ds(m, 128)
        value = dot3(bh[at, :], bl[at, :], rh[...], rl[...])
        to = pl.ds(pl.multiple_of(y * 384 + m, 128), 128)
        p_sums[0] = p_sums[0] + col_sum(value[:, :128] * r_s[0, to, :])
        p_sums[1] = p_sums[1] + col_sum(value[:, 128:] * w_half[at, :])

    def add_rows(p, first):
        row = pl.ds(pl.multiple_of(p * 384, 384), 384)
        for c in range(2):
            split_to(r_s[1 + c, row, :], rh, rl, row, 128 * c)
        cols = pl.ds(pl.multiple_of(p * 384, 128), 384)
        for m in range(0, 384, 128):
            at = pl.ds(m, 128)
            value = dot3(bh[at, cols], bl[at, cols], rh[row, :], rl[row, :])
            acc[at, :] = value if first else acc[at, :] + value

    add_rows(y, True)
    for c in range(2):
        ring_r[c].near()
    add_rows(lax.rem(y + 1, 4), False)
    add_rows(lax.rem(y + 3, 4), False)
    for c in range(2):
        ring_r[c].far()
    add_rows(lax.rem(y + 2, 4), False)
    c_sums = [e_sums[c] + v_sums[:, c * 128:(c + 1) * 128] for c in range(2)]
    for m in range(0, 384, 128):
        to = pl.ds(pl.multiple_of(y * 384 + m, 128), 128)
        for c in range(2):
            c_sums[c] = c_sums[c] + col_sum(acc[pl.ds(m, 128), c * 128:(c + 1) * 128] * r_s[1 + c, to, :])

    for c in range(2):
        stage[c:c + 1, :] = p_sums[c]
        stage[2 + c:3 + c, :] = c_sums[c]
    stage[4:8, :] = jnp.zeros((4, 128), F32)
    fin[y] = stage[...]
    ends = [remote(stage, fin.at[y], at_y(lax.rem(y + d, 4))) for d in (1, 3, 2)]
    for copy in ends:
        copy.start()
    for copy in ends:
        copy.wait_recv()
    ostage[...] = ((fin[0] + fin[1]) + fin[2]) + fin[3]
    place = 4 * group + col
    xfin[place] = ostage[...]
    ends = [remote(ostage, xfin.at[place], peer) for peer in row_peers]
    for copy in ends:
        copy.start()
    for copy in ends:
        copy.wait_recv()
    before = 2 - mine[2] - mine[3]
    for j in range(4):
        own, other = xfin[4 * core + j], xfin[4 - 4 * core + j]
        out[8 + 2 * j:9 + 2 * j, :] = select(mine[0], own[2:3], select(before, other[3:4], other[2:3]))
        out[9 + 2 * j:10 + 2 * j, :] = select(mine[1], select(mine[0], own[3:4], own[2:3]), other[3:4])
        t = (0, 2, 3, 5)[j]
        out[t:t + 1, :] = own[0:1]
        if j in (0, 2):
            after = xfin[4 * core + j + 1]
            out[t + 1:t + 2, :] = pack(own[1:2], after[1:2])
    out[6:8, :] = jnp.zeros((2, 128), F32)
    for copy in copies:
        copy.wait_send()

    @pl.when(hub)
    def _():
        for copy in hub_copies:
            copy.wait_send()

    for j in range(4):
        @pl.when(jnp.logical_not(is_own[j]))
        def _(j=j):
            for copy in e_across[j] + d_across[j]:
                copy.wait_send()


COPIES = 160


def shards(b, f, d, cf, e, idx, owner):
    vm = pltpu.VMEM
    any_spec = pl.BlockSpec(memory_space=pl.ANY)
    vmem_spec = pl.BlockSpec(memory_space=pltpu.VMEM)
    out = pl.pallas_call(
        kernel,
        out_shape=jax.ShapeDtypeStruct((16, 128), F32),
        in_specs=[any_spec] * 7,
        out_specs=vmem_spec,
        scratch_shapes=[
            vm((2, 2, 32, 512), F32), vm((2, 2, 64, 512), F32), vm((2, 32, 512), F32), vm((2, 64, 512), F32),
            vm((384, 1536), F32), vm((384, 768), F32), vm((192, 768), F32),
            vm((2, 256, 512), F32), vm((2, 512, 128), F32), vm((2, 192, 128), F32),
            vm((2, 1024, 128), F32), vm((768, 128), F32), vm((384, 128), F32),
            vm((3, 1536, 128), F32), vm((384, 128), F32), vm((768, 128), F32),
            vm((4, 384, 128), F32), vm((4, 192, 128), F32),
            vm((8, 1024), jnp.int32), vm((384, 256), F32), vm((384, 256), F32),
            pltpu.SMEM((64,), jnp.int32),
            vm((2, 768, 1024), BF16), vm((2, 384, 1024), BF16),
            vm((384, 1536), BF16), vm((384, 1536), BF16),
            vm((384, 768), BF16), vm((384, 768), BF16),
            vm((192, 768), BF16), vm((192, 768), BF16),
            vm((2, 256, 512), BF16), vm((2, 256, 512), BF16),
            vm((2, 512, 128), BF16), vm((2, 512, 128), BF16),
            vm((2, 1024, 128), BF16), vm((2, 1024, 128), BF16),
            vm((768, 256), BF16), vm((768, 256), BF16),
            vm((768, 256), BF16), vm((768, 256), BF16),
            vm((384, 768), BF16), vm((384, 768), BF16),
            vm((1536, 256), BF16), vm((1536, 256), BF16),
            vm((8, 128), F32), vm((4, 8, 128), F32), vm((8, 128), F32), vm((8, 8, 128), F32),
            pltpu.SemaphoreType.DMA((COPIES,)),
            pltpu.SemaphoreType.DMA((COPIES,)),
            pltpu.SemaphoreType.DMA((11,)),
        ],
        compiler_params=pltpu.CompilerParams(
            collective_id=0, has_side_effects=True, vmem_limit_bytes=60 * 1024 * 1024
        ),
        name="selected",
    )(b[0], f[0], d[0], cf, e, idx, owner)
    kids = out[8:16].reshape(4, 2, 128).transpose(1, 0, 2).reshape(2, 512)
    return out[0:6].reshape(1, 768), kids


def solution(mesh):
    split_spec = P("leaf", "front", None)
    in_specs = (split_spec,) * 5 + (P(), P())
    out_specs = (P("leaf", None), P("leaf", None))
    return jax.shard_map(shards, mesh=mesh, in_specs=in_specs, out_specs=out_specs, check_vma=False)
```

time: 83.3 us -> 73.7 us (0.88)
  Pallas kernels: 80.6 us -> 70.9 us
    pallas_call x1, Pallas kernels: 80.6 us -> 70.9 us  [shards(): pl.pallas_call(kernel, out_shape=jax.ShapeDtypeStruct((16, 128), F32), in...]
where the time goes in v3:
time: 73.7 us; the launch traced here: 73.5 us
  Pallas kernels  70.9 us (96%)
  local copies, waits for them, and re-layouts  1.92 us (3%)
    pallas_call x1, Pallas kernels, shards(): pl.pallas_call(kernel, out_shape=jax.ShapeDtypeStruct((16, 128), F32), in...  70.9 us

profile of v3, /device:TPU:1, one launch (start us, length us, event | category | flops | bytes accessed | tf_op | source)
XLA Modules:
  0.0 73.5 jit_solution(6165587068085632439)
XLA Ops:
  0.6 70.9 %selected.1 = f32[16,128]{1,0:T(8,128)} custom-call(f32[96,1536]{1,0:T(8,128)} %bitcast.14, f32[96,768]{1,0:T(8,128)} %bitcast.15, f32[48,768]{1,0:T(8,128)} %bitcast.16, f32[2,64,512]{2,1,0:T(8,128)} %cf_in.1, f32[2,32,512]{2,1,0:T(8,128)} %e_in.1, s32[64,1024]{1,0:T(8,128)} %idx_in.1, s32[64]{0:T(128)} %owner_in.1), custom_call_target="tpu_custom_call" | custom-call | tf_op jit(solution)/shard_map/selected/pallas_call | solution.py:570
  71.6 0.0 copy-start
  71.6 0.7 %slice_bitcast_fusion = f32[1,1,6,128]{3,2,1,0:T(8,128)S(1)} fusion(f32[16,128]{1,0:T(8,128)} %selected.1), kind=kLoop, calls=%fused_computation | loop fusion | bytes 6144
  72.3 0.6 copy.12
  72.9 0.0 copy-done
  72.9 0.6 slice.7
Async XLA Ops:
  71.6 1.3 %copy-start = (f32[16,128]{1,0:T(8,128)S(1)}, f32[16,128]{1,0:T(8,128)}, u32[]{:S(2)}) copy-start(f32[16,128]{1,0:T(8,128)} %selected.1) | copy-start | bytes 24580

commit v4 on v3

v4 whole, which is shorter than its diff:
```python
import jax
import jax.numpy as jnp
from jax import lax
from jax.experimental import pallas as pl
from jax.experimental.pallas import tpu as pltpu
from jax.sharding import PartitionSpec as P

F32 = jnp.float32
BF16 = jnp.bfloat16
MESH = pl.DeviceIdType.MESH


def dot(a, b):
    return jnp.dot(a, b, preferred_element_type=F32)


def dot3(ah, al, bh, bl):
    return dot(ah, bh) + (dot(ah, bl) + dot(al, bh))


def split(x):
    hi = x.astype(BF16)
    return hi, (x - hi.astype(F32)).astype(BF16)


def col_sum(x):
    return jnp.sum(x, axis=0, keepdims=True)


def select(flag, yes, no):
    return jnp.where(jnp.full(yes.shape, flag, jnp.int32) == 1, yes, no)


def kernel(
    b_in, f_in, d_in, cf_in, e_in, idx_in, owner_in,
    out_p, out_d, out_c, out_e,
    e_raw, c_raw, e_sel, c_sel,
    b_s, f_s, d_s, cf_s, e_s, k_s, v_s, r_s, w_half, w_s, w_x,
    idx_s, l_s, acc, owner,
    su, sl, bh, bl, fh, fl, dh, dl, ch, cl, eh, el, kh, kl, uh, ul, vh, vl, wh, wl, rh, rl,
    stage, fin, ostage, xfin, send, recv, loc,
):
    leaf = lax.axis_index("leaf")
    front = lax.axis_index("front")
    y = lax.div(front, 4)
    x = lax.rem(front, 4)
    core = lax.rem(leaf, 2)
    base = leaf - core
    partner = base + 1 - core
    group = lax.div(x, 2)
    pair = x + 1 - 2 * lax.rem(x, 2)
    col = 2 * lax.rem(x, 2) + core
    hub = core == group
    taken = [0, 0]

    def sends():
        taken[0] += 1
        return send.at[taken[0] - 1]

    def arrivals(n=1):
        taken[1] += n
        return recv.at[taken[1] - 1] if n == 1 else taken[1] - n

    def remote(src, dst, device, sent, arrived):
        return pltpu.make_async_remote_copy(
            src_ref=src, dst_ref=dst, send_sem=sent, recv_sem=arrived,
            device_id=device, device_id_type=MESH,
        )

    def wait(ref, sem):
        pltpu.make_async_copy(ref, ref, sem).wait()

    def at_y(p):
        return {"front": p * 4 + x}

    def on(chip, a_core=None):
        if a_core is None:
            return {"front": y * 4 + chip}
        return {"leaf": base + a_core, "front": y * 4 + chip}

    other_core = {"leaf": partner}

    rings, matrices = [], []

    class Ring:
        def __init__(self, part, span):
            right, left = lax.rem(y + 1, 4), lax.rem(y + 3, 4)
            self.span, self.sent = span, sends()
            self.near_sem, self.far_sem = arrivals(), arrivals()
            self.right = [
                remote(part(y, h), part(y, h), at_y(right), self.sent, at)
                for h, at in ((0, arrivals()), (1, self.near_sem))
            ]
            self.left = [
                remote(part(y, h), part(y, h), at_y(left), self.sent, at)
                for h, at in ((1, arrivals()), (0, self.near_sem))
            ]
            self.next_right = remote(part(left, 0), part(left, 0), at_y(right), self.sent, self.far_sem)
            self.next_left = remote(part(right, 1), part(right, 1), at_y(left), self.sent, self.far_sem)
            rings.append(self)

        def begin(self):
            for h in range(2):
                self.right[h].start()
                self.left[h].start()

        def relay(self):
            self.right[0].wait_recv()
            self.next_right.start()
            self.left[0].wait_recv()
            self.next_left.start()

        def near(self):
            wait(self.span(1), self.near_sem)

        def far(self):
            wait(self.span(1), self.far_sem)

        def finish(self):
            self.near()
            self.far()

        def end(self):
            wait(self.span(3), self.sent)

    class Rows:
        def __init__(self, part, whole, full, src, own, sem):
            self.whole, self.full = whole, full
            first = arrivals(3)
            goal = jnp.where(hub, pair, 3 - x)
            self.first_sent, self.next_sent, self.inside_sent = sends(), sends(), sends()
            self.pair_sem, self.next_sem, self.inside_sem = recv.at[first], arrivals(), arrivals()
            self.first = [
                remote(src(h), part(x, h), on(goal), self.first_sent, recv.at[first + jnp.where(hub, 0, 1 + h)])
                for h in (0, 1)
            ]
            self.far_in = [(part(3 - x, h), recv.at[first + 1 + h]) for h in (0, 1)]
            self.next = [
                remote(part(3 - x, h), part(3 - x, h), on(pair), self.next_sent, self.next_sem)
                for h in (0, 1)
            ]
            self.inside = [
                remote(whole(p), whole(p), other_core, self.inside_sent, self.inside_sem)
                for p in (x, 3 - x, pair, 3 - pair)
            ]
            self.local = pltpu.make_async_copy(own, whole(x), loc.at[sem])
            matrices.append(self)

        def begin(self):
            for h in range(2):
                self.first[h].start()

            @pl.when(hub)
            def _():
                self.local.start()

        def relay(self):
            @pl.when(hub)
            def _():
                self.local.wait()
                self.inside[0].start()
                for h in range(2):
                    wait(*self.far_in[h])
                    self.next[h].start()
                self.inside[1].start()

        def near(self):
            @pl.when(hub)
            def _():
                wait(self.whole(pair), self.pair_sem)
                self.inside[2].start()

        def pass_on(self):
            @pl.when(hub)
            def _():
                wait(self.whole(3 - pair), self.next_sem)
                self.inside[3].start()

        def finish(self):
            @pl.when(jnp.logical_not(hub))
            def _():
                wait(self.full, self.inside_sem)

        def end(self):
            wait(self.whole(0), self.first_sent)

            @pl.when(hub)
            def _():
                wait(self.whole(0), self.next_sent)
                wait(self.full, self.inside_sent)

    def halves(ref, size, *lead):
        return lambda p, h: ref.at[(*lead, pl.ds(p * size + h * (size // 2), size // 2), slice(None))]

    def wholes(ref, size, *lead):
        return lambda p: ref.at[(*lead, pl.ds(p * size, size), slice(None))]

    def span(ref, size, *lead):
        return lambda n: ref.at[(*lead, pl.ds(0, size * n), slice(None))]

    def of(ref, size, lane=slice(None)):
        return lambda h: ref.at[pl.ds(h * (size // 2), size // 2), lane]

    lanes_768 = [pl.ds(0, 768), pl.ds(768, 768)]

    barrier = pltpu.get_barrier_semaphore()
    peers = [at_y(lax.rem(y + d, 4)) for d in (1, 2, 3)]
    row_peers = [on(lax.rem(x + d, 4), core) for d in (1, 3, 2)]
    row_peers += [on(lax.rem(x + d, 4), 1 - core) for d in (0, 1, 3, 2)]
    for peer in peers + row_peers:
        pl.semaphore_signal(barrier, inc=1, device_id=peer, device_id_type=MESH)

    def lanes(t):
        return pl.ds(pl.multiple_of(t * 128, 128), 128)

    def tiles(p):
        return lanes(p + lax.div(p + 1, 2)), lanes(1 + 3 * lax.div(p, 2))

    full_tile, half_tile = tiles(col)
    moves = [
        (idx_in.at[pl.ds(pl.multiple_of(lax.div(leaf, 4) * 8, 8), 8), :], idx_s),
        (owner_in, owner),
        (e_in, e_raw.at[0]),
        (cf_in, c_raw.at[0]),
    ]
    moves = [pltpu.make_async_copy(src, dst, loc.at[i]) for i, (src, dst) in enumerate(moves)]
    own_idx, own_owner, own_e, own_cf = moves
    for copy in (own_owner, own_e, own_cf, own_idx):
        copy.start()

    e_cross = remote(e_in, e_raw.at[1], other_core, sends(), arrivals())
    c_cross = remote(cf_in, c_raw.at[1], other_core, sends(), arrivals())

    def e_rows(p):
        return e_s.at[:, pl.ds(y * 128 + p * 32, 32), :]

    e_at = arrivals(4)
    e_across, is_own = [], []
    for j in range(4):
        is_own.append(jnp.logical_and(hub, col == j))
        e_across.append(remote(
            e_sel.at[:, :, lanes(j)], e_rows(x), on(2 * core + j // 2, j % 2), sends(), recv.at[e_at + x]
        ))
    e_kept = pltpu.make_async_copy(e_sel.at[:, :, lanes(col)], e_rows(x), loc.at[4])

    rows_d = Rows(halves(d_s, 48), wholes(d_s, 48), d_s, of(d_in, 48), d_in, 5)
    rows_c = Rows(
        lambda p, h: cf_s.at[h, pl.ds(p * 64, 64), :], lambda p: cf_s.at[:, pl.ds(p * 64, 64), :], cf_s,
        lambda h: c_sel.at[h], c_sel, 6,
    )
    rows_f = Rows(halves(f_s, 96), wholes(f_s, 96), f_s, of(f_in, 96), f_in, 7)
    rows_b = [
        Rows(halves(b_s, 96, c), wholes(b_s, 96, c), b_s.at[c], of(b_in, 96, lanes_768[c]), b_in.at[:, lanes_768[c]], 8 + c)
        for c in range(2)
    ]
    ring_e = Ring(lambda p, h: e_s.at[h, pl.ds(p * 128, 128), :], lambda n: e_s.at[:, pl.ds(0, 128 * n), :])
    ring_dp = Ring(halves(v_s, 288), span(v_s, 288))
    ring_k = [Ring(halves(k_s, 256, c), span(k_s, 256, c)) for c in range(2)]
    ring_w = Ring(halves(w_s, 576), span(w_s, 576))
    ring_r = [Ring(halves(r_s, 384, c), span(r_s, 384, c)) for c in range(2)]
    w_pair = remote(w_x.at[col], w_x.at[col], on(pair), sends(), arrivals())
    w_in = remote(w_x.at[col], w_x.at[col], other_core, sends(), arrivals())
    far_col = 2 * lax.rem(pair, 2) + core
    w_on = remote(w_x.at[far_col], w_x.at[far_col], other_core, sends(), arrivals())

    pl.semaphore_wait(barrier, 10)

    e_cross.start()
    c_cross.start()
    rows_d.begin()

    def members(mine_leaf, other_leaf):
        pool = (2 * mine_leaf, 2 * mine_leaf + 1, 2 * other_leaf, 2 * other_leaf + 1)
        return pool, [(owner[p] == mine_leaf).astype(jnp.int32) for p in pool]

    def pick(c, flags, items):
        if c == 0:
            return select(flags[0], items[0], select(flags[1], items[1], items[2]))
        return select(flags[3], items[3], select(flags[2], items[2], items[1]))

    own_owner.wait()
    _, mine = members(leaf, partner)
    pool, held = members(base + group, base + 1 - group)
    own_e.wait()
    e_cross.wait_recv()
    for c in range(2):
        e_sel[c] = pick(c, mine, [e_raw[0, 0], e_raw[0, 1], e_raw[1, 0], e_raw[1, 1]])

    @pl.when(hub)
    def _():
        e_kept.start()

    for j in (2, 3, 0, 1):
        @pl.when(jnp.logical_not(is_own[j]))
        def _(j=j):
            e_across[j].start()

    rows_d.relay()
    own_cf.wait()
    c_cross.wait_recv()
    for c in range(2):
        for m in (0, 32):
            at = pl.ds(m, 32)
            c_sel[c, at, :] = pick(
                c, mine, [c_raw[0, 0, at, :], c_raw[0, 1, at, :], c_raw[1, 0, at, :], c_raw[1, 1, at, :]]
            )
    rows_c.begin()
    rows_d.near()

    own_idx.wait()
    idx_rows = [idx_s[pl.ds(lax.rem(p, 8), 1), :] for p in pool]

    def one_hot(c):
        positions = pick(c, held, idx_rows)
        for m in range(0, 768, 128):
            at = lax.broadcasted_iota(jnp.int32, (128, 1024), 0) + m
            su[c, pl.ds(m, 128), :] = jnp.where(at == positions, 1.0, 0.0).astype(BF16)
        for m in range(0, 384, 128):
            at = lax.broadcasted_iota(jnp.int32, (128, 1024), 0) + (768 + 384 * y + m)
            sl[c, pl.ds(m, 128), :] = jnp.where(at == positions, 1.0, 0.0).astype(BF16)

    def split_rows(src, hi, lo, size, step):
        for m in range(0, size, step):
            h, l = split(src[pl.ds(m, step), :])
            hi[pl.ds(m, step), :] = h
            lo[pl.ds(m, step), :] = l

    def split_to(value, hi, lo, row, lane):
        h, l = split(value)
        hi[row, pl.ds(lane, 128)] = h
        lo[row, pl.ds(lane, 128)] = l

    def low_lanes(shape):
        return lax.broadcasted_iota(jnp.int32, shape, 1) < 64

    def swap(value):
        return pltpu.roll(value, 64, 1)

    def pack(top, bottom):
        return jnp.where(low_lanes(top.shape), top, swap(bottom))

    @pl.when(hub)
    def _():
        e_kept.wait()

    for p in range(4):
        @pl.when(jnp.logical_not(jnp.logical_and(hub, x == p)))
        def _(p=p):
            wait(e_rows(p), recv.at[e_at + p])

    ring_e.begin()
    rows_d.pass_on()
    rows_c.relay()
    rows_f.begin()
    ring_e.relay()

    rows_d.finish()
    whole = d_s[:, full_tile]
    half = d_s[:, half_tile]
    half = select(core, swap(half), half)
    d_sums = [col_sum(whole * whole), col_sum(half * half)]
    v_s[pl.ds(pl.multiple_of(y * 288, 96), 192), :] = whole
    v_s[pl.ds(pl.multiple_of(y * 288 + 192, 96), 96), :] = pack(half[:96], half[96:])
    ring_dp.begin()
    one_hot(0)
    rows_c.near()

    ring_e.finish()
    e_sums = []
    for c in range(2):
        for m in range(0, 512, 128):
            h, l = split(e_s[c, pl.ds(m, 128), :])
            eh[c, pl.ds(m, 128), :] = h
            el[c, pl.ds(m, 128), :] = l
        part = e_s[c, pl.ds(pl.multiple_of(y * 128, 128), 128), :]
        e_sums.append(col_sum(part * part))
    rows_f.relay()
    rows_c.pass_on()
    rows_c.finish()
    ring_dp.relay()
    for c in range(2):
        for m in range(0, 256, 64):
            h, l = split(cf_s[c, pl.ds(m, 64), :])
            ch[c, pl.ds(m, 64), :] = h
            cl[c, pl.ds(m, 64), :] = l
        for m in range(0, 256, 128):
            at = pl.ds(m, 128)
            k_s[c, pl.ds(pl.multiple_of(y * 256 + m, 128), 128), :] = dot3(ch[c, at, :], cl[c, at, :], eh[c], el[c])
        ring_k[c].begin()
    rows_b[0].begin()
    rows_f.near()
    one_hot(1)
    split_rows(d_s, dh, dl, 192, 48)

    ring_dp.finish()
    for p in range(4):
        for m in (0, 96):
            split_to(v_s[pl.ds(288 * p + m, 96), :], vh, vl, pl.ds(192 * p + m, 96), 0)
            value = v_s[pl.ds(288 * p + 192, 96), :]
            split_to(swap(value) if m else value, vh, vl, pl.ds(192 * p + m, 96), 128)
    ring_k[0].relay()
    rows_f.pass_on()
    rows_f.finish()
    split_rows(f_s, fh, fl, 384, 48)
    for m in (0, 192):
        at = pl.ds(m, 192)
        value = dot3(fh[at, :], fl[at, :], vh[...], vl[...])
        w_s[pl.ds(pl.multiple_of(y * 576 + m, 192), 192), :] = value[:, :128]
        w_x[col, at, :] = value[:, :128]
        w_half[at, :] = value[:, 128:]
    packed = pack(w_half[0:192, :], w_half[192:384, :])
    w_s[pl.ds(pl.multiple_of(y * 576 + 384, 192), 192), :] = packed
    w_x[col, pl.ds(384, 192), :] = packed
    w_pair.start()
    w_in.start()
    ring_k[1].relay()
    ring_w.begin()
    rows_b[0].relay()
    rows_b[1].begin()

    for c in range(2):
        ring_k[c].finish()
        for m in range(0, 1024, 128):
            h, l = split(k_s[c, pl.ds(m, 128), :])
            kh[c, pl.ds(m, 128), :] = h
            kl[c, pl.ds(m, 128), :] = l
        for m in range(0, 768, 256):
            at = pl.ds(m, 256)
            uh[at, pl.ds(c * 128, 128)] = dot(su[c, at, :], kh[c]).astype(BF16)
            ul[at, pl.ds(c * 128, 128)] = dot(su[c, at, :], kl[c]).astype(BF16)
        if c == 0:
            ring_w.relay()
        else:
            w_pair.wait_recv()
            w_on.start()
        for m in range(0, 384, 128):
            at = pl.ds(m, 128)
            l_s[at, pl.ds(c * 128, 128)] = dot(sl[c, at, :], kh[c]) + dot(sl[c, at, :], kl[c])

    rows_b[0].near()
    rows_b[1].relay()
    w_in.wait_recv()
    w_on.wait_recv()
    for p, t in enumerate((0, 2, 3, 5)):
        for m in (0, 192):
            split_to(w_x[p, pl.ds(m, 192), :], wh, wl, pl.ds(m, 192), 128 * t)
    for p, t in ((0, 1), (2, 4)):
        low, high = w_x[p, pl.ds(384, 192), :], w_x[p + 1, pl.ds(384, 192), :]
        split_to(jnp.where(low_lanes(low.shape), low, swap(high)), wh, wl, pl.ds(0, 192), 128 * t)
        split_to(jnp.where(low_lanes(low.shape), swap(low), high), wh, wl, pl.ds(192, 192), 128 * t)
    for c in range(2):
        cols = pl.ds(c * 128, 128)
        for m in (0, 192):
            at = pl.ds(m, 192)
            value = l_s[at, cols] - dot3(wh[at, :], wl[at, :], uh[:, cols], ul[:, cols])
            r_s[c, pl.ds(pl.multiple_of(y * 384 + m, 192), 192), :] = value
        ring_r[c].begin()
    rows_b[0].pass_on()
    rows_b[1].near()
    value = dot3(dh[...], dl[...], uh[...], ul[...])
    v_sums = col_sum(value * value)
    ring_r[0].relay()
    rows_b[1].pass_on()
    ring_r[1].relay()
    ring_w.finish()
    for c in range(2):
        rows_b[c].finish()
        split_rows(b_s.at[c], bh.at[:, lanes_768[c]], bl.at[:, lanes_768[c]], 384, 48)

    for p in range(4):
        for m in (0, 192):
            row = pl.ds(p * 384 + m, 192)
            split_to(w_s[pl.ds(p * 576 + m, 192), :], rh, rl, row, 0)
            value = w_s[pl.ds(p * 576 + 384, 192), :]
            split_to(swap(value) if m else value, rh, rl, row, 128)
    p_sums = [jnp.zeros((1, 128), F32)] * 2
    for m in range(0, 384, 128):
        at = pl.ds(m, 128)
        value = dot3(bh[at, :], bl[at, :], rh[...], rl[...])
        to = pl.ds(pl.multiple_of(y * 576 + m, 64), 128)
        p_sums[0] = p_sums[0] + col_sum(value[:, :128] * w_s[to, :])
        p_sums[1] = p_sums[1] + col_sum(value[:, 128:] * w_half[at, :])

    def add_rows(p, first):
        row = pl.ds(pl.multiple_of(p * 384, 384), 384)
        for c in range(2):
            split_to(r_s[c, row, :], rh, rl, row, 128 * c)
        cols = pl.ds(pl.multiple_of(p * 384, 128), 384)
        for m in range(0, 384, 128):
            at = pl.ds(m, 128)
            value = dot3(bh[at, cols], bl[at, cols], rh[row, :], rl[row, :])
            acc[at, :] = value if first else acc[at, :] + value

    add_rows(y, True)
    for c in range(2):
        ring_r[c].near()
    add_rows(lax.rem(y + 1, 4), False)
    add_rows(lax.rem(y + 3, 4), False)
    for c in range(2):
        ring_r[c].far()
    add_rows(lax.rem(y + 2, 4), False)
    c_sums = [v_sums[:, c * 128:(c + 1) * 128] for c in range(2)]
    for m in range(0, 384, 128):
        to = pl.ds(pl.multiple_of(y * 384 + m, 128), 128)
        for c in range(2):
            c_sums[c] = c_sums[c] + col_sum(acc[pl.ds(m, 128), c * 128:(c + 1) * 128] * r_s[c, to, :])

    for c in range(2):
        stage[c:c + 1, :] = p_sums[c]
        stage[2 + c:3 + c, :] = c_sums[c]
        stage[4 + c:5 + c, :] = d_sums[c]
        stage[6 + c:7 + c, :] = e_sums[c]
    fin[y] = stage[...]
    sent, arrived = sends(), arrivals()
    for d in (1, 3, 2):
        remote(stage, fin.at[y], at_y(lax.rem(y + d, 4)), sent, arrived).start()
    wait(fin.at[pl.ds(0, 3)], arrived)
    ostage[...] = ((fin[0] + fin[1]) + fin[2]) + fin[3]
    place = 4 * group + col
    xfin[place] = ostage[...]
    last_sent, arrived = sends(), arrivals()
    for peer in row_peers:
        remote(ostage, xfin.at[place], peer, last_sent, arrived).start()
    wait(xfin.at[pl.ds(0, 7)], arrived)
    before = 2 - mine[2] - mine[3]
    for j, t in enumerate((0, 2, 3, 5)):
        own, other = xfin[4 * core + j], xfin[4 - 4 * core + j]
        for ref, r in ((out_c, 2), (out_e, 6)):
            first = select(before, other[r + 1:r + 2], other[r:r + 1])
            ref[0:1, j * 128:(j + 1) * 128] = select(mine[0], own[r:r + 1], first)
            second = select(mine[0], own[r + 1:r + 2], own[r:r + 1])
            ref[1:2, j * 128:(j + 1) * 128] = select(mine[1], second, other[r + 1:r + 2])
        for ref, r in ((out_p, 0), (out_d, 4)):
            ref[:, t * 128:(t + 1) * 128] = own[r:r + 1]
            if j in (0, 2):
                after = xfin[4 * core + j + 1]
                ref[:, (t + 1) * 128:(t + 2) * 128] = pack(own[r + 1:r + 2], after[r + 1:r + 2])
    for each in rings + matrices:
        each.end()
    for copy in [e_cross, c_cross, w_pair, w_in, w_on]:
        copy.wait_send()
    for j in range(4):
        @pl.when(jnp.logical_not(is_own[j]))
        def _(j=j):
            e_across[j].wait_send()

    wait(fin.at[pl.ds(0, 3)], sent)
    wait(xfin.at[pl.ds(0, 7)], last_sent)
    assert taken == [SENDS, ARRIVALS], taken


SENDS, ARRIVALS = 33, 64


def shards(b, f, d, cf, e, idx, owner):
    vm = pltpu.VMEM
    any_spec = pl.BlockSpec(memory_space=pl.ANY)
    vmem_spec = pl.BlockSpec(memory_space=pltpu.VMEM)
    row, kid = jax.ShapeDtypeStruct((1, 768), F32), jax.ShapeDtypeStruct((2, 512), F32)
    quad_p, diag_p, quad_c, diag_c = pl.pallas_call(
        kernel,
        out_shape=(row, row, kid, kid),
        in_specs=[any_spec] * 7,
        out_specs=(vmem_spec,) * 4,
        scratch_shapes=[
            vm((2, 2, 32, 512), F32), vm((2, 2, 64, 512), F32), vm((2, 32, 512), F32), vm((2, 64, 512), F32),
            vm((2, 384, 768), F32), vm((384, 768), F32), vm((192, 768), F32),
            vm((2, 256, 512), F32), vm((2, 512, 128), F32),
            vm((2, 1024, 128), F32), vm((1152, 128), F32),
            vm((2, 1536, 128), F32), vm((384, 128), F32), vm((2304, 128), F32), vm((4, 576, 128), F32),
            vm((8, 1024), jnp.int32), vm((384, 256), F32), vm((384, 256), F32),
            pltpu.SMEM((64,), jnp.int32),
            vm((2, 768, 1024), BF16), vm((2, 384, 1024), BF16),
            vm((384, 1536), BF16), vm((384, 1536), BF16),
            vm((384, 768), BF16), vm((384, 768), BF16),
            vm((192, 768), BF16), vm((192, 768), BF16),
            vm((2, 256, 512), BF16), vm((2, 256, 512), BF16),
            vm((2, 512, 128), BF16), vm((2, 512, 128), BF16),
            vm((2, 1024, 128), BF16), vm((2, 1024, 128), BF16),
            vm((768, 256), BF16), vm((768, 256), BF16),
            vm((768, 256), BF16), vm((768, 256), BF16),
            vm((384, 768), BF16), vm((384, 768), BF16),
            vm((1536, 256), BF16), vm((1536, 256), BF16),
            vm((8, 128), F32), vm((4, 8, 128), F32), vm((8, 128), F32), vm((8, 8, 128), F32),
            pltpu.SemaphoreType.DMA((SENDS,)),
            pltpu.SemaphoreType.DMA((ARRIVALS,)),
            pltpu.SemaphoreType.DMA((10,)),
        ],
        compiler_params=pltpu.CompilerParams(
            collective_id=0, has_side_effects=True, vmem_limit_bytes=60 * 1024 * 1024
        ),
        name="selected",
    )(b[0], f[0], d[0], cf, e, idx, owner)
    return diag_p + quad_p, diag_c + quad_c


def solution(mesh):
    split_spec = P("leaf", "front", None)
    in_specs = (split_spec,) * 5 + (P(), P())
    out_specs = (P("leaf", None), P("leaf", None))
    return jax.shard_map(shards, mesh=mesh, in_specs=in_specs, out_specs=out_specs, check_vma=False)
```

time: 73.7 us -> 70.8 us (0.961)
  Pallas kernels: 70.9 us -> 68 us
  other arithmetic: 0 us -> 1.18 us
  local copies, waits for them, and re-layouts: 1.92 us -> 0.78 us
    pallas_call x1, Pallas kernels: 70.9 us -> 68 us  [shards(): pl.pallas_call(kernel, out_shape=(row, row, kid, kid), in_specs=[any_spec...]
    add x0 -> x2, other arithmetic: none -> 1.18 us  [shards(): return (diag_p + quad_p, diag_c + quad_c)]
where the time goes in v4:
time: 70.8 us; the launch traced here: 70.7 us
  Pallas kernels  68 us (96%)
  other arithmetic  1.18 us (2%)
  local copies, waits for them, and re-layouts  0.78 us (1%)
    pallas_call x1, Pallas kernels, shards(): pl.pallas_call(kernel, out_shape=(row, row, kid, kid), in_specs=[any_spec...  68 us

profile of v4, /device:TPU:1, one launch (start us, length us, event | category | flops | bytes accessed | tf_op | source)
XLA Modules:
  0.0 70.7 jit_solution(16029410878954397763)
XLA Ops:
  0.6 68.0 %selected.1 = (f32[1,768]{1,0:T(1,128)}, f32[1,768]{1,0:T(1,128)}, f32[2,512]{1,0:T(2,128)}, f32[2,512]{1,0:T(2,128)}) custom-call(f32[96,1536]{1,0:T(8,128)} %bitcast.3, f32[96,768]{1,0:T(8,128)} %bitcast.4, f32[48,768]{1,0:T(8,128)} %bitcast.5, f32[2,64,512]{2,1,0:T(8,128)} %cf_in.1, f32[2,32,512]{2,1,0:T(8,128)} %e_in.1, s32[64,1024]{1,0:T(8,128)} %idx_in.1, ...), custom_call_target="tpu_custom_call" | custom-call | tf_op jit(solution)/shard_map/selected/pallas_call | solution.py:560
  68.7 0.0 copy-start.3
  68.7 0.0 copy-start.2
  68.7 0.7 copy-done.3
  69.3 0.0 copy-done.2
  69.4 0.0 copy-start
  69.4 0.0 copy-start.1
  69.4 0.6 add.6
  70.0 0.1 copy-done
  70.0 0.0 copy-done.1
  70.1 0.6 add.7
Async XLA Ops:
  68.7 0.7 copy-start.3
  68.7 0.7 copy-start.2
  69.4 0.7 copy-start
  69.4 0.7 copy-start.1

commit v5 on v4

--- a/solution.py
+++ b/solution.py
@@ -35,9 +35,9 @@
     b_in, f_in, d_in, cf_in, e_in, idx_in, owner_in,
     out_p, out_d, out_c, out_e,
     e_raw, c_raw, e_sel, c_sel,
-    b_s, f_s, d_s, cf_s, e_s, k_s, v_s, r_s, w_half, w_s, w_x,
-    idx_s, l_s, acc, owner,
-    su, sl, bh, bl, fh, fl, dh, dl, ch, cl, eh, el, kh, kl, uh, ul, vh, vl, wh, wl, rh, rl,
+    b_s, f_s, d_s, cf_s, e_s, k_s, v_s, u_s, w_half, w_s, w_x,
+    idx_s, r_own, acc, owner,
+    place, bh, bl, fh, fl, dh, dl, ch, cl, eh, el, kk, uh, ul, vh, vl, wh, wl, rh, rl, lh, ll,
     stage, fin, ostage, xfin, send, recv, loc,
 ):
     leaf = lax.axis_index("leaf")
@@ -257,11 +257,16 @@
     ring_dp = Ring(halves(v_s, 288), span(v_s, 288))
     ring_k = [Ring(halves(k_s, 256, c), span(k_s, 256, c)) for c in range(2)]
     ring_w = Ring(halves(w_s, 576), span(w_s, 576))
-    ring_r = [Ring(halves(r_s, 384, c), span(r_s, 384, c)) for c in range(2)]
-    w_pair = remote(w_x.at[col], w_x.at[col], on(pair), sends(), arrivals())
-    w_in = remote(w_x.at[col], w_x.at[col], other_core, sends(), arrivals())
+    ring_v = Ring(
+        lambda p, h: u_s.at[h, pl.ds(p * 192, 192), :], lambda n: u_s.at[:, pl.ds(0, 192 * n), :]
+    )
     far_col = 2 * lax.rem(pair, 2) + core
-    w_on = remote(w_x.at[far_col], w_x.at[far_col], other_core, sends(), arrivals())
+    w_pair, w_in, w_on = [], [], []
+    for rows in (pl.ds(0, 384), pl.ds(384, 192)):
+        near, far = w_x.at[col, rows, :], w_x.at[far_col, rows, :]
+        w_pair.append(remote(near, near, on(pair), sends(), arrivals()))
+        w_in.append(remote(near, near, other_core, sends(), arrivals()))
+        w_on.append(remote(far, far, other_core, sends(), arrivals()))
 
     pl.semaphore_wait(barrier, 10)
 
@@ -312,12 +317,9 @@
 
     def one_hot(c):
         positions = pick(c, held, idx_rows)
-        for m in range(0, 768, 128):
+        for m in range(0, 2304, 128):
             at = lax.broadcasted_iota(jnp.int32, (128, 1024), 0) + m
-            su[c, pl.ds(m, 128), :] = jnp.where(at == positions, 1.0, 0.0).astype(BF16)
-        for m in range(0, 384, 128):
-            at = lax.broadcasted_iota(jnp.int32, (128, 1024), 0) + (768 + 384 * y + m)
-            sl[c, pl.ds(m, 128), :] = jnp.where(at == positions, 1.0, 0.0).astype(BF16)
+            place[c, pl.ds(m, 128), :] = jnp.where(at == positions, 1.0, 0.0).astype(BF16)
 
     def split_rows(src, hi, lo, size, step):
         for m in range(0, size, step):
@@ -406,62 +408,45 @@
         at = pl.ds(m, 192)
         value = dot3(fh[at, :], fl[at, :], vh[...], vl[...])
         w_s[pl.ds(pl.multiple_of(y * 576 + m, 192), 192), :] = value[:, :128]
-        w_x[col, at, :] = value[:, :128]
         w_half[at, :] = value[:, 128:]
     packed = pack(w_half[0:192, :], w_half[192:384, :])
     w_s[pl.ds(pl.multiple_of(y * 576 + 384, 192), 192), :] = packed
-    w_x[col, pl.ds(384, 192), :] = packed
-    w_pair.start()
-    w_in.start()
     ring_k[1].relay()
     ring_w.begin()
     rows_b[0].relay()
     rows_b[1].begin()
 
+    v_sums = []
     for c in range(2):
         ring_k[c].finish()
         for m in range(0, 1024, 128):
             h, l = split(k_s[c, pl.ds(m, 128), :])
-            kh[c, pl.ds(m, 128), :] = h
-            kl[c, pl.ds(m, 128), :] = l
+            kk[c, pl.ds(m, 128), pl.ds(0, 128)] = h
+            kk[c, pl.ds(m, 128), pl.ds(128, 128)] = l
+        cols = pl.ds(c * 128, 128)
         for m in range(0, 768, 256):
             at = pl.ds(m, 256)
-            uh[at, pl.ds(c * 128, 128)] = dot(su[c, at, :], kh[c]).astype(BF16)
-            ul[at, pl.ds(c * 128, 128)] = dot(su[c, at, :], kl[c]).astype(BF16)
+            value = dot(place[c, at, :], kk[c]).astype(BF16)
+            uh[at, cols] = value[:, :128]
+            ul[at, cols] = value[:, 128:]
         if c == 0:
             ring_w.relay()
-        else:
-            w_pair.wait_recv()
-            w_on.start()
-        for m in range(0, 384, 128):
-            at = pl.ds(m, 128)
-            l_s[at, pl.ds(c * 128, 128)] = dot(sl[c, at, :], kh[c]) + dot(sl[c, at, :], kl[c])
-
-    rows_b[0].near()
-    rows_b[1].relay()
-    w_in.wait_recv()
-    w_on.wait_recv()
-    for p, t in enumerate((0, 2, 3, 5)):
-        for m in (0, 192):
-            split_to(w_x[p, pl.ds(m, 192), :], wh, wl, pl.ds(m, 192), 128 * t)
-    for p, t in ((0, 1), (2, 4)):
-        low, high = w_x[p, pl.ds(384, 192), :], w_x[p + 1, pl.ds(384, 192), :]
-        split_to(jnp.where(low_lanes(low.shape), low, swap(high)), wh, wl, pl.ds(0, 192), 128 * t)
-        split_to(jnp.where(low_lanes(low.shape), swap(low), high), wh, wl, pl.ds(192, 192), 128 * t)
-    for c in range(2):
-        cols = pl.ds(c * 128, 128)
-        for m in (0, 192):
-            at = pl.ds(m, 192)
-            value = l_s[at, cols] - dot3(wh[at, :], wl[at, :], uh[:, cols], ul[:, cols])
-            r_s[c, pl.ds(pl.multiple_of(y * 384 + m, 192), 192), :] = value
-        ring_r[c].begin()
+            rows_b[0].near()
+            rows_b[1].relay()
+        value = dot3(dh[...], dl[...], uh[:, cols], ul[:, cols])
+        u_s[c, pl.ds(pl.multiple_of(y * 192, 192), 192), :] = value
+        v_sums.append(col_sum(value * value))
+    ring_v.begin()
     rows_b[0].pass_on()
     rows_b[1].near()
-    value = dot3(dh[...], dl[...], uh[...], ul[...])
-    v_sums = col_sum(value * value)
-    ring_r[0].relay()
+    for c in range(2):
+        cols = pl.ds(c * 128, 128)
+        for m in range(0, 1536, 256):
+            at = pl.ds(m, 256)
+            value = dot(place[c, pl.ds(768 + m, 256), :], kk[c]).astype(BF16)
+            lh[at, cols] = value[:, :128]
+            ll[at, cols] = value[:, 128:]
     rows_b[1].pass_on()
-    ring_r[1].relay()
     ring_w.finish()
     for c in range(2):
         rows_b[c].finish()
@@ -480,30 +465,45 @@
         to = pl.ds(pl.multiple_of(y * 576 + m, 64), 128)
         p_sums[0] = p_sums[0] + col_sum(value[:, :128] * w_s[to, :])
         p_sums[1] = p_sums[1] + col_sum(value[:, 128:] * w_half[at, :])
-
-    def add_rows(p, first):
-        row = pl.ds(pl.multiple_of(p * 384, 384), 384)
-        for c in range(2):
-            split_to(r_s[c, row, :], rh, rl, row, 128 * c)
-        cols = pl.ds(pl.multiple_of(p * 384, 128), 384)
-        for m in range(0, 384, 128):
-            at = pl.ds(m, 128)
-            value = dot3(bh[at, cols], bl[at, cols], rh[row, :], rl[row, :])
-            acc[at, :] = value if first else acc[at, :] + value
-
-    add_rows(y, True)
-    for c in range(2):
-        ring_r[c].near()
-    add_rows(lax.rem(y + 1, 4), False)
-    add_rows(lax.rem(y + 3, 4), False)
-    for c in range(2):
-        ring_r[c].far()
-    add_rows(lax.rem(y + 2, 4), False)
-    c_sums = [v_sums[:, c * 128:(c + 1) * 128] for c in range(2)]
+        w_x[col, at, :] = value[:, :128]
+        w_half[at, :] = value[:, 128:]
+    w_x[col, pl.ds(384, 192), :] = pack(w_half[0:192, :], w_half[192:384, :])
+    for n in range(2):
+        w_pair[n].start()
+        w_in[n].start()
+    ring_v.relay()
+
     for m in range(0, 384, 128):
+        at = pl.ds(m, 128)
+        acc[at, :] = dot3(bh[at, :], bl[at, :], lh[...], ll[...])
+    ring_v.finish()
+    for c in range(2):
+        for m in range(0, 768, 128):
+            split_to(u_s[c, pl.ds(m, 128), :], vh, vl, pl.ds(m, 128), 128 * c)
+    for m in range(0, 384, 128):
+        at = pl.ds(m, 128)
         to = pl.ds(pl.multiple_of(y * 384 + m, 128), 128)
-        for c in range(2):
-            c_sums[c] = c_sums[c] + col_sum(acc[pl.ds(m, 128), c * 128:(c + 1) * 128] * r_s[c, to, :])
+        value = lh[to, :].astype(F32) + ll[to, :].astype(F32)
+        r_own[at, :] = value - dot3(fh[at, :], fl[at, :], vh[...], vl[...])
+    for n in range(2):
+        w_pair[n].wait_recv()
+        w_on[n].start()
+    for n in range(2):
+        w_in[n].wait_recv()
+        w_on[n].wait_recv()
+    for p, t in enumerate((0, 2, 3, 5)):
+        for m in (0, 192):
+            split_to(w_x[p, pl.ds(m, 192), :], wh, wl, pl.ds(m, 192), 128 * t)
+    for p, t in ((0, 1), (2, 4)):
+        low, high = w_x[p, pl.ds(384, 192), :], w_x[p + 1, pl.ds(384, 192), :]
+        split_to(jnp.where(low_lanes(low.shape), low, swap(high)), wh, wl, pl.ds(0, 192), 128 * t)
+        split_to(jnp.where(low_lanes(low.shape), swap(low), high), wh, wl, pl.ds(192, 192), 128 * t)
+    c_sums = v_sums
+    for m in range(0, 384, 128):
+        at = pl.ds(m, 128)
+        value = acc[at, :] - dot3(wh[at, :], wl[at, :], uh[...], ul[...])
+        value = col_sum(value * r_own[at, :])
+        c_sums = [c_sums[c] + value[:, c * 128:(c + 1) * 128] for c in range(2)]
 
     for c in range(2):
         stage[c:c + 1, :] = p_sums[c]
@@ -516,11 +516,11 @@
         remote(stage, fin.at[y], at_y(lax.rem(y + d, 4)), sent, arrived).start()
     wait(fin.at[pl.ds(0, 3)], arrived)
     ostage[...] = ((fin[0] + fin[1]) + fin[2]) + fin[3]
-    place = 4 * group + col
-    xfin[place] = ostage[...]
+    my_place = 4 * group + col
+    xfin[my_place] = ostage[...]
     last_sent, arrived = sends(), arrivals()
     for peer in row_peers:
-        remote(ostage, xfin.at[place], peer, last_sent, arrived).start()
+        remote(ostage, xfin.at[my_place], peer, last_sent, arrived).start()
     wait(xfin.at[pl.ds(0, 7)], arrived)
     before = 2 - mine[2] - mine[3]
     for j, t in enumerate((0, 2, 3, 5)):
@@ -537,7 +537,7 @@
                 ref[:, (t + 1) * 128:(t + 2) * 128] = pack(own[r + 1:r + 2], after[r + 1:r + 2])
     for each in rings + matrices:
         each.end()
-    for copy in [e_cross, c_cross, w_pair, w_in, w_on]:
+    for copy in [e_cross, c_cross] + w_pair + w_in + w_on:
         copy.wait_send()
     for j in range(4):
         @pl.when(jnp.logical_not(is_own[j]))
@@ -549,7 +549,7 @@
     assert taken == [SENDS, ARRIVALS], taken
 
 
-SENDS, ARRIVALS = 33, 64
+SENDS, ARRIVALS = 35, 63
 
 
 def shards(b, f, d, cf, e, idx, owner):
@@ -567,19 +567,20 @@
             vm((2, 384, 768), F32), vm((384, 768), F32), vm((192, 768), F32),
             vm((2, 256, 512), F32), vm((2, 512, 128), F32),
             vm((2, 1024, 128), F32), vm((1152, 128), F32),
-            vm((2, 1536, 128), F32), vm((384, 128), F32), vm((2304, 128), F32), vm((4, 576, 128), F32),
+            vm((2, 768, 128), F32), vm((384, 128), F32), vm((2304, 128), F32), vm((4, 576, 128), F32),
             vm((8, 1024), jnp.int32), vm((384, 256), F32), vm((384, 256), F32),
             pltpu.SMEM((64,), jnp.int32),
-            vm((2, 768, 1024), BF16), vm((2, 384, 1024), BF16),
+            vm((2, 2304, 1024), BF16),
             vm((384, 1536), BF16), vm((384, 1536), BF16),
             vm((384, 768), BF16), vm((384, 768), BF16),
             vm((192, 768), BF16), vm((192, 768), BF16),
             vm((2, 256, 512), BF16), vm((2, 256, 512), BF16),
             vm((2, 512, 128), BF16), vm((2, 512, 128), BF16),
-            vm((2, 1024, 128), BF16), vm((2, 1024, 128), BF16),
+            vm((2, 1024, 256), BF16),
             vm((768, 256), BF16), vm((768, 256), BF16),
             vm((768, 256), BF16), vm((768, 256), BF16),
             vm((384, 768), BF16), vm((384, 768), BF16),
+            vm((1536, 256), BF16), vm((1536, 256), BF16),
             vm((1536, 256), BF16), vm((1536, 256), BF16),
             vm((8, 128), F32), vm((4, 8, 128), F32), vm((8, 128), F32), vm((8, 8, 128), F32),
             pltpu.SemaphoreType.DMA((SENDS,)),

time: 70.8 us -> 69 us (0.975)
  Pallas kernels: 68 us -> 66.2 us
    pallas_call x1, Pallas kernels: 68 us -> 66.2 us  [shards(): pl.pallas_call(kernel, out_shape=(row, row, kid, kid), in_specs=[any_spec...]
where the time goes in v5:
time: 69 us; the launch traced here: 68.8 us
  Pallas kernels  66.2 us (96%)
  other arithmetic  1.18 us (2%)
  local copies, waits for them, and re-layouts  0.78 us (1%)
    pallas_call x1, Pallas kernels, shards(): pl.pallas_call(kernel, out_shape=(row, row, kid, kid), in_specs=[any_spec...  66.2 us

profile of v5, /device:TPU:1, one launch (start us, length us, event | category | flops | bytes accessed | tf_op | source)
XLA Modules:
  0.0 68.8 jit_solution(1970593636460279580)
XLA Ops:
  0.6 66.2 %selected.1 = (f32[1,768]{1,0:T(1,128)}, f32[1,768]{1,0:T(1,128)}, f32[2,512]{1,0:T(2,128)}, f32[2,512]{1,0:T(2,128)}) custom-call(f32[96,1536]{1,0:T(8,128)} %bitcast.3, f32[96,768]{1,0:T(8,128)} %bitcast.4, f32[48,768]{1,0:T(8,128)} %bitcast.5, f32[2,64,512]{2,1,0:T(8,128)} %cf_in.1, f32[2,32,512]{2,1,0:T(8,128)} %e_in.1, s32[64,1024]{1,0:T(8,128)} %idx_in.1, ...), custom_call_target="tpu_custom_call" | custom-call | tf_op jit(solution)/shard_map/selected/pallas_call | solution.py:560
  66.8 0.0 copy-start.3
  66.8 0.0 copy-start.2
  66.9 0.7 copy-done.3
  67.5 0.0 copy-done.2
  67.5 0.0 copy-start
  67.5 0.0 copy-start.1
  67.5 0.6 add.6
  68.1 0.1 copy-done
  68.2 0.0 copy-done.1
  68.2 0.6 add.7
Async XLA Ops:
  66.8 0.7 copy-start.3
  66.8 0.7 copy-start.2
  67.5 0.7 copy-start
  67.5 0.7 copy-start.1

commit v6 on v5

--- a/solution.py
+++ b/solution.py
@@ -129,20 +129,22 @@
             first = arrivals(3)
             goal = jnp.where(hub, pair, 3 - x)
             self.first_sent, self.next_sent, self.inside_sent = sends(), sends(), sends()
-            self.pair_sem, self.next_sem, self.inside_sem = recv.at[first], arrivals(), arrivals()
+            self.pair_sem, self.next_sems, self.inside_sem = recv.at[first], [arrivals(), arrivals()], arrivals()
             self.first = [
                 remote(src(h), part(x, h), on(goal), self.first_sent, recv.at[first + jnp.where(hub, 0, 1 + h)])
                 for h in (0, 1)
             ]
             self.far_in = [(part(3 - x, h), recv.at[first + 1 + h]) for h in (0, 1)]
             self.next = [
-                remote(part(3 - x, h), part(3 - x, h), on(pair), self.next_sent, self.next_sem)
+                remote(part(3 - x, h), part(3 - x, h), on(pair), self.next_sent, self.next_sems[h])
                 for h in (0, 1)
             ]
             self.inside = [
                 remote(whole(p), whole(p), other_core, self.inside_sent, self.inside_sem)
-                for p in (x, 3 - x, pair, 3 - pair)
+                for p in (x, 3 - x, pair)
             ]
+            self.last_in = [part(3 - pair, h) for h in (0, 1)]
+            self.inside += [remote(ref, ref, other_core, self.inside_sent, self.inside_sem) for ref in self.last_in]
             self.local = pltpu.make_async_copy(own, whole(x), loc.at[sem])
             matrices.append(self)
 
@@ -173,8 +175,9 @@
         def pass_on(self):
             @pl.when(hub)
             def _():
-                wait(self.whole(3 - pair), self.next_sem)
-                self.inside[3].start()
+                for h in range(2):
+                    wait(self.last_in[h], self.next_sems[h])
+                    self.inside[3 + h].start()
 
         def finish(self):
             @pl.when(jnp.logical_not(hub))
@@ -262,7 +265,7 @@
     )
     far_col = 2 * lax.rem(pair, 2) + core
     w_pair, w_in, w_on = [], [], []
-    for rows in (pl.ds(0, 384), pl.ds(384, 192)):
+    for rows in (pl.ds(0, 128), pl.ds(128, 128), pl.ds(256, 128), pl.ds(384, 192)):
         near, far = w_x.at[col, rows, :], w_x.at[far_col, rows, :]
         w_pair.append(remote(near, near, on(pair), sends(), arrivals()))
         w_in.append(remote(near, near, other_core, sends(), arrivals()))
@@ -447,30 +450,40 @@
             lh[at, cols] = value[:, :128]
             ll[at, cols] = value[:, 128:]
     rows_b[1].pass_on()
-    ring_w.finish()
-    for c in range(2):
+
+    def split_w(p):
+        for m in (0, 192):
+            row = pl.ds(pl.multiple_of(p * 384 + m, 192), 192)
+            split_to(w_s[pl.ds(pl.multiple_of(p * 576 + m, 192), 192), :], rh, rl, row, 0)
+            value = w_s[pl.ds(pl.multiple_of(p * 576 + 384, 192), 192), :]
+            split_to(swap(value) if m else value, rh, rl, row, 128)
+
+    def split_b(c):
         rows_b[c].finish()
         split_rows(b_s.at[c], bh.at[:, lanes_768[c]], bl.at[:, lanes_768[c]], 384, 48)
 
-    for p in range(4):
-        for m in (0, 192):
-            row = pl.ds(p * 384 + m, 192)
-            split_to(w_s[pl.ds(p * 576 + m, 192), :], rh, rl, row, 0)
-            value = w_s[pl.ds(p * 576 + 384, 192), :]
-            split_to(swap(value) if m else value, rh, rl, row, 128)
+    split_b(0)
+    split_w(y)
+    ring_w.near()
+    split_w(lax.rem(y + 1, 4))
+    split_w(lax.rem(y + 3, 4))
+    split_b(1)
+    ring_w.far()
+    split_w(lax.rem(y + 2, 4))
     p_sums = [jnp.zeros((1, 128), F32)] * 2
-    for m in range(0, 384, 128):
-        at = pl.ds(m, 128)
+    for n in range(3):
+        at = pl.ds(128 * n, 128)
         value = dot3(bh[at, :], bl[at, :], rh[...], rl[...])
-        to = pl.ds(pl.multiple_of(y * 576 + m, 64), 128)
+        w_x[col, at, :] = value[:, :128]
+        w_pair[n].start()
+        w_in[n].start()
+        to = pl.ds(pl.multiple_of(y * 576 + 128 * n, 64), 128)
         p_sums[0] = p_sums[0] + col_sum(value[:, :128] * w_s[to, :])
         p_sums[1] = p_sums[1] + col_sum(value[:, 128:] * w_half[at, :])
-        w_x[col, at, :] = value[:, :128]
         w_half[at, :] = value[:, 128:]
     w_x[col, pl.ds(384, 192), :] = pack(w_half[0:192, :], w_half[192:384, :])
-    for n in range(2):
-        w_pair[n].start()
-        w_in[n].start()
+    w_pair[3].start()
+    w_in[3].start()
     ring_v.relay()
 
     for m in range(0, 384, 128):
@@ -485,10 +498,10 @@
         to = pl.ds(pl.multiple_of(y * 384 + m, 128), 128)
         value = lh[to, :].astype(F32) + ll[to, :].astype(F32)
         r_own[at, :] = value - dot3(fh[at, :], fl[at, :], vh[...], vl[...])
-    for n in range(2):
+    for n in range(4):
         w_pair[n].wait_recv()
         w_on[n].start()
-    for n in range(2):
+    for n in range(4):
         w_in[n].wait_recv()
         w_on[n].wait_recv()
     for p, t in enumerate((0, 2, 3, 5)):
@@ -549,7 +562,7 @@
     assert taken == [SENDS, ARRIVALS], taken
 
 
-SENDS, ARRIVALS = 35, 63
+SENDS, ARRIVALS = 41, 74
 
 
 def shards(b, f, d, cf, e, idx, owner):

time: 69 us -> 68.2 us (0.988)
  Pallas kernels: 66.2 us -> 65.4 us
    pallas_call x1, Pallas kernels: 66.2 us -> 65.4 us  [shards(): pl.pallas_call(kernel, out_shape=(row, row, kid, kid), in_specs=[any_spec...]
where the time goes in v6:
time: 68.2 us; the launch traced here: 68.1 us
  Pallas kernels  65.4 us (96%)
  other arithmetic  1.18 us (2%)
  local copies, waits for them, and re-layouts  0.78 us (1%)
    pallas_call x1, Pallas kernels, shards(): pl.pallas_call(kernel, out_shape=(row, row, kid, kid), in_specs=[any_spec...  65.4 us

profile of v6, /device:TPU:1, one launch (start us, length us, event | category | flops | bytes accessed | tf_op | source)
XLA Modules:
  0.0 68.1 jit_solution(10975793284618364314)
XLA Ops:
  0.6 65.4 %selected.1 = (f32[1,768]{1,0:T(1,128)}, f32[1,768]{1,0:T(1,128)}, f32[2,512]{1,0:T(2,128)}, f32[2,512]{1,0:T(2,128)}) custom-call(f32[96,1536]{1,0:T(8,128)} %bitcast.3, f32[96,768]{1,0:T(8,128)} %bitcast.4, f32[48,768]{1,0:T(8,128)} %bitcast.5, f32[2,64,512]{2,1,0:T(8,128)} %cf_in.1, f32[2,32,512]{2,1,0:T(8,128)} %e_in.1, s32[64,1024]{1,0:T(8,128)} %idx_in.1, ...), custom_call_target="tpu_custom_call" | custom-call | tf_op jit(solution)/shard_map/selected/pallas_call | solution.py:573
  66.1 0.0 copy-start.3
  66.1 0.0 copy-start.2
  66.1 0.7 copy-done.3
  66.7 0.0 copy-done.2
  66.8 0.0 copy-start
  66.8 0.0 copy-start.1
  66.8 0.6 add.6
  67.4 0.1 copy-done
  67.4 0.0 copy-done.1
  67.5 0.6 add.7
Async XLA Ops:
  66.1 0.7 copy-start.3
  66.1 0.7 %copy-start.2 = (f32[1,768]{1,0:T(1,128)S(1)}, f32[1,768]{1,0:T(1,128)}, u32[]{:S(2)}) copy-start(f32[1,768]{1,0:T(1,128)} %get-tuple-element.7) | copy-start | bytes 9220
  66.8 0.7 copy-start
  66.8 0.7 %copy-start.1 = (f32[2,512]{1,0:T(2,128)S(1)}, f32[2,512]{1,0:T(2,128)}, u32[]{:S(2)}) copy-start(f32[2,512]{1,0:T(2,128)} %get-tuple-element.8) | copy-start | bytes 12292
